TPU v7x, 32 devices: a whole 2x2x4 slice. The times are simulated.
32 devices in a mesh: groups: 2 (over x), ty: 4 (over y, core), tx: 4 (over z).
Axes of the slice: x: 2, y: 2, z: 4, core: 2. Of those that a mesh axis runs over, the one named last changes fastest.
Arguments:
- object_planes: float32 [4, 2048, 1024], P(None, ('groups', 'ty'), 'tx'), parts along dimension 1, may hold values from -5 to 5
- probe: float32 [2, 256, 256], replicated, may hold values from -5 to 5
- phase: float32 [256, 256], replicated, may hold values from -3.140625 to 3.140625
- coords: int32 [8, 4, 4, 2], P(('groups', 'ty'), 'tx'), parts along dimension 0, may hold values from 0 to 255
- live: int32 [8, 4], P(('groups', 'ty'), 'tx'), parts along dimension 0, may hold values from 0 to 4, as said below
- amplitude: float32 [8, 4, 4, 256, 256], P(('groups', 'ty'), 'tx'), parts along dimension 0, may hold values from 0 to 2
Outputs:
- updated: float32 [4, 2048, 1024], P(None, ('groups', 'ty'), 'tx'), parts along dimension 1
There are 2 independent parts, one for each index of `groups`. A program takes and returns all parts, laid end to end along the dimension named above; an argument that names none is the same for every part. Nothing has to cross between parts.
Inputs may be any that keep to these rules, and one draw needn't show every extreme that they name: Only slots below live of their tile are used; some tile holds 4 live slots.
All inputs are finite; a program needn't handle non-finite values.
Results may differ from a plain program's by a relative error of at most 0.0003.
Values sent between devices are 32-bit elements; how exact they have to be, the bound alone decides.
A program may use at most 128 MiB of HBM per device.

v0:
```python
import math

import jax
import jax.numpy as jnp
from jax import lax
from jax.sharding import PartitionSpec as P

HIGH = lax.Precision.HIGHEST


def from_behind(block, axis, distance):
    devices = range(lax.axis_size(axis))
    route = [(i - distance, i) for i in devices if i - distance in devices]
    return lax.ppermute(block, axis, route)


def dft_tables(probe_width):
    index_grid = (
        jnp.arange(probe_width, dtype=jnp.int32)[:, None]
        * jnp.arange(probe_width, dtype=jnp.int32)[None, :]
        % probe_width
    )
    angles = index_grid.astype(jnp.float32) * (2.0 * math.pi / probe_width)
    norm_scale = 1.0 / math.sqrt(probe_width)
    return (jnp.cos(angles) * norm_scale, -jnp.sin(angles) * norm_scale)


def product(left_mat, right_mat):
    return jnp.dot(left_mat, right_mat, precision=HIGH, preferred_element_type=jnp.float32)


def transform(real_part, imag_part, cos_table, sin_table):
    left_r = product(cos_table, real_part) - product(sin_table, imag_part)
    left_i = product(cos_table, imag_part) + product(sin_table, real_part)
    out_r = product(left_r, cos_table) - product(left_i, sin_table)
    out_i = product(left_r, sin_table) + product(left_i, cos_table)
    return (out_r, out_i)


def slot_terms(probe, phase_r, phase_i, cos_table, sin_table, patch, amp_plane):
    probe_r, probe_i = (probe[0], probe[1])
    first_r, first_i, second_r, second_i = (patch[0], patch[1], patch[2], patch[3])
    wave_one_r = probe_r * first_r - probe_i * first_i
    wave_one_i = probe_r * first_i + probe_i * first_r
    spec_r, spec_i = transform(wave_one_r, wave_one_i, cos_table, sin_table)
    moved_r = spec_r * phase_r - spec_i * phase_i
    moved_i = spec_r * phase_i + spec_i * phase_r
    wave_two_r, wave_two_i = transform(moved_r, moved_i, cos_table, -sin_table)
    exit_r = wave_two_r * second_r - wave_two_i * second_i
    exit_i = wave_two_r * second_i + wave_two_i * second_r
    far_r, far_i = transform(exit_r, exit_i, cos_table, sin_table)
    ratio = amp_plane / jnp.maximum(jnp.sqrt(far_r * far_r + far_i * far_i), 0.5) - 1.0
    back_r, back_i = transform(far_r * ratio, far_i * ratio, cos_table, -sin_table)
    grad_two_r = wave_two_r * back_r + wave_two_i * back_i
    grad_two_i = wave_two_r * back_i - wave_two_i * back_r
    inner_r = second_r * back_r + second_i * back_i
    inner_i = second_r * back_i - second_i * back_r
    turn_r, turn_i = transform(inner_r, inner_i, cos_table, sin_table)
    undo_r = turn_r * phase_r + turn_i * phase_i
    undo_i = turn_i * phase_r - turn_r * phase_i
    prior_r, prior_i = transform(undo_r, undo_i, cos_table, -sin_table)
    grad_one_r = probe_r * prior_r + probe_i * prior_i
    grad_one_i = probe_r * prior_i - probe_i * prior_r
    power_two = wave_two_r * wave_two_r + wave_two_i * wave_two_i
    return jnp.stack([grad_one_r, grad_one_i, grad_two_r, grad_two_i, power_two])


def on_device(object_planes, probe, phase, coords, live, amplitude):
    probe_width = probe.shape[-1]
    slot_count = coords.shape[2]
    half_slots = slot_count // 2
    cos_table, sin_table = dft_tables(probe_width)
    phase_r, phase_i = (jnp.cos(phase), jnp.sin(phase))
    zero_index = jnp.int32(0)
    right_part = from_behind(object_planes, "tx", -1)
    band_rows = jnp.concatenate([object_planes, right_part], axis=2)
    lower_part = from_behind(band_rows, "ty", -1)
    region = jnp.concatenate([band_rows, lower_part], axis=1)
    offsets = coords[0, 0]

    def extract(where_yx):
        return lax.dynamic_slice(
            region, (zero_index, where_yx[0], where_yx[1]), (4, probe_width, probe_width)
        )

    patches = jax.vmap(extract)(offsets)
    slot_items = jnp.concatenate([patches, amplitude[0, 0][:, None]], axis=1)
    blank_rows = jnp.zeros((half_slots, 5, probe_width, probe_width), jnp.float32)
    working = jnp.concatenate([blank_rows, slot_items, blank_rows])
    own_count = live[0, 0]

    def process(count_now, working):
        results = jnp.zeros_like(working)

        def handle(slot_index, results):
            slot_data = lax.dynamic_index_in_dim(
                working, slot_index + half_slots, 0, keepdims=False
            )
            gradients = slot_terms(
                probe, phase_r, phase_i, cos_table, sin_table, slot_data[0:4], slot_data[4]
            )
            return lax.dynamic_update_index_in_dim(results, gradients, slot_index + half_slots, 0)

        return lax.fori_loop(zero_index, count_now, handle, results)

    results = process(own_count, working)
    probe_power = probe[0] * probe[0] + probe[1] * probe[1]
    totals = jnp.zeros((6, 2 * probe_width, 2 * probe_width), jnp.float32)

    def deposit(slot_index, totals):
        where_yx = lax.dynamic_index_in_dim(offsets, slot_index, 0, keepdims=False)
        gradients = lax.dynamic_index_in_dim(results, slot_index + half_slots, 0, keepdims=False)
        contrib = jnp.concatenate([gradients[0:2], probe_power[None], gradients[2:5]])
        current = lax.dynamic_slice(
            totals, (zero_index, where_yx[0], where_yx[1]), (6, probe_width, probe_width)
        )
        return lax.dynamic_update_slice(
            totals, current + contrib, (zero_index, where_yx[0], where_yx[1])
        )

    totals = lax.fori_loop(zero_index, own_count, deposit, totals)
    lower_sums = from_behind(totals[:, probe_width:, :], "ty", 1)
    upper_rows = totals[:, :probe_width, :] + lower_sums
    right_sums = from_behind(upper_rows[:, :, probe_width:], "tx", 1)
    own_sums = upper_rows[:, :, :probe_width] + right_sums
    first = object_planes[0:2] + own_sums[0:2] / (own_sums[2:3] + 1.0)
    second = object_planes[2:4] + own_sums[3:5] / (own_sums[5:6] + 1.0)
    return jnp.concatenate([first, second])


def solution(mesh):
    return jax.shard_map(
        on_device,
        mesh=mesh,
        in_specs=(
            P(None, ("groups", "ty"), "tx"),
            P(),
            P(),
            P(("groups", "ty"), "tx", None, None),
            P(("groups", "ty"), "tx"),
            P(("groups", "ty"), "tx", None, None, None),
        ),
        out_specs=P(None, ("groups", "ty"), "tx"),
        check_vma=False,
    )
```

profile of v0, /device:TPU:22, one launch (start us, length us, event | category | flops | bytes accessed | tf_op | source)
XLA Modules:
  0.0 585.6 jit_solution(6684838528119378348)
XLA Ops:
  0.0 2.5 collective-permute-start
  2.5 2.4 constant_dynamic-update-slice_fusion.1
  4.9 22.3 %collective-permute-done = f32[4,256,256]{2,1,0:T(8,128)S(1)} collective-permute-done((f32[4,256,256]{2,1,0:T(8,128)}, f32[4,256,256]{2,1,0:T(8,128)S(1)}, u32[]{:S(2)}, u32[]{:S(2)}) %collective-permute-start) | collective-permute-done | bytes 1048608 | tf_op jit(solution)/shard_map/ppermute | solution.py:14
  28.3 1.9 collective-permute-start.1
  30.4 1.9 fusion.305
  32.3 21.8 %collective-permute-done.1 = f32[4,256,512]{2,1,0:T(8,128)S(1)} collective-permute-done((f32[4,256,512]{2,1,0:T(8,128)}, f32[4,256,512]{2,1,0:T(8,128)S(1)}, u32[]{:S(2)}, u32[]{:S(2)}) %collective-permute-start.1) | collective-permute-done | bytes 2097184 | tf_op jit(solution)/shard_map/ppermute | solution.py:14
  54.0 4.0 pad_maximum_fusion.1
  58.0 19.0 %while.28 = (s32[]{:T(128)}, f32[4,512,512]{2,1,0:T(8,128)}, s32[4,3]{1,0:T(4,128)S(1)}, f32[4,4,256,256]{3,2,1,0:T(8,128)}, s32[]{:T(128)}) while((s32[]{:T(128)}, f32[4,512,512]{2,1,0:T(8,128)}, s32[4,3]{1,0:T(4,128)S(1)}, f32[4,4,256,256]{3,2,1,0:T(8,128)}, s32[]{:T(128)}) %tuple.98), condition=%wide.while_cond, body=%wide.while_body.sunk | while | flops 2 | bytes 2098793 | solution.py:82
  58.7 4.1 bitcast_dynamic-update-slice_fusion.14
  63.4 4.1 bitcast_dynamic-update-slice_fusion.14
  68.2 4.1 bitcast_dynamic-update-slice_fusion.14
  73.0 4.1 bitcast_dynamic-update-slice_fusion.14
  78.3 6.0 %pad_maximum_fusion = f32[8,5,256,256]{3,2,1,0:T(8,128)} fusion(f32[2,5,256,256]{3,2,1,0:T(8,128)S(1)} %broadcast_in_dim.28, f32[4,1,256,256]{3,2,1,0:T(8,128)S(1)} %bitcast.287, f32[4,4,256,256]{3,2,1,0:T(8,128)} %get-tuple-element.352), kind=kLoop, calls=%fused_computation.346 | loop fusion | flops 7864320 | bytes 18350080 | tf_op jit(solution)/shard_map/concatenate | solution.py:89
  84.3 5.1 broadcast_in_dim.27
  89.4 84.8 %while.29 = (s32[]{:T(128)}, f32[8,5,256,256]{3,2,1,0:T(8,128)}, s32[]{:T(128)}, f32[2,256,256]{2,1,0:T(8,128)S(1)}, f32[8,5,256,256]{3,2,1,0:T(8,128)}, /*index...) while((s32[]{:T(128)}, f32[8,5,256,256]{3,2,1,0:T(8,128)}, ...), condition=%wide.region_1.2_spmd.clone.clone, body=%wide.region_0.1_spmd.clone.clone.sunk | while | flops 9718398976 | bytes 47972628 | solution.py:104
  93.0 1.5 convolution_add_fusion.20
  96.0 1.5 convolution_subtract_fusion.22
  98.9 1.5 convolution_subtract_fusion.23
  100.4 1.5 fusion.502
  101.9 2.1 multiply_add_fusion.6
  105.5 1.5 convolution_add_fusion.21
  108.4 1.5 convolution_subtract_fusion.24
  114.4 2.7 multiply_add_fusion.7
  118.5 1.5 convolution_add_fusion.22
  121.5 1.5 convolution_subtract_fusion.26
  127.4 2.7 fusion.511
  130.1 1.5 fusion.514
  131.6 1.5 convolution_add_fusion.23
  133.1 1.5 fusion.512
  134.6 1.5 convolution_subtract_fusion.28
  136.1 1.5 fusion.513
  137.6 1.5 convolution_add_fusion.24
  140.6 3.0 multiply_subtract_fusion.6
  145.1 1.5 convolution_add_fusion.25
  148.0 1.5 convolution_subtract_fusion.29
  149.5 1.5 fusion.517
  154.0 1.7 multiply_subtract_fusion.7
  157.1 1.5 convolution_add_fusion.27
  160.1 1.5 convolution_subtract_fusion.30
  174.3 3.5 broadcast_in_dim.26
  177.7 27.4 %while.27 = (s32[]{:T(128)}, f32[6,512,512]{2,1,0:T(8,128)}, s32[]{:T(128)}, s32[4,2]{0,1:T(2,128)S(1)}, f32[8,5,256,256]{3,2,1,0:T(8,128)}, /*index=5*/f32[256,...) while((s32[]{:T(128)}, f32[6,512,512]{2,1,0:T(8,128)}, ...), condition=%wide.region_3.4_spmd, body=%wide.region_2.3_spmd.sunk | while | flops 1179664 | bytes 10486105 | solution.py:121
  185.1 2.2 maximum_add_fusion.2
  187.3 17.2 %dynamic_update_slice.18 = f32[6,512,512]{2,1,0:T(8,128)} dynamic-update-slice(f32[6,512,512]{2,1,0:T(8,128)} %get-tuple-element.732, f32[6,256,256]{2,1,0:T(8,128)S(1)} %maximum_add_fusion.2, s32[]{:T(128)} %constant.96.clone.1..sunk, s32[]{:T(128)S(6)} %select_n.290, s32[]{:T(128)S(6)} %select_n.291) | dynamic-update-slice | bytes 3145732 | tf_op jit(solution)/shard_map/while/body/dynamic_update_slice | solution.py:117
  205.2 2.4 slice.137
  207.5 2.1 collective-permute-start.2
  209.6 36.7 %collective-permute-done.2 = f32[6,256,512]{2,1,0:T(8,128)S(1)} collective-permute-done((f32[6,256,512]{2,1,0:T(8,128)S(1)}, f32[6,256,512]{2,1,0:T(8,128)S(1)}, u32[]{:S(2)}, u32[]{:S(2)}) %collective-permute-start.2) | collective-permute-done | bytes 3145760 | tf_op jit(solution)/shard_map/ppermute | solution.py:14
  247.2 318.6 %collective-permute-start.3 = (f32[6,256,256]{2,1,0:T(8,128)S(1)}, f32[6,256,256]{2,1,0:T(8,128)S(1)}, u32[]{:S(2)}, u32[]{:S(2)}) collective-permute-start(f32[6,256,256]{2,1,0:T(8,128)S(1)} %slice.175), channel_id=1, source_target_pairs={{0,1},{1,2},{2,3},{4,5},{5,6},{6,7},{8,9},{9,10},{10,11},{12,13},{... | collective-permute-start | bytes 4718600 | tf_op jit(solution)/shard_map/ppermute | solution.py:14
  565.9 17.9 %collective-permute-done.3 = f32[6,256,256]{2,1,0:T(8,128)S(1)} collective-permute-done((f32[6,256,256]{2,1,0:T(8,128)S(1)}, f32[6,256,256]{2,1,0:T(8,128)S(1)}, u32[]{:S(2)}, u32[]{:S(2)}) %collective-permute-start.3) | collective-permute-done | bytes 1572896 | tf_op jit(solution)/shard_map/ppermute | solution.py:14
  (66 shorter events, 48.3 us)
Async XLA Ops:
  0.0 30.2 %copy-start.4 = (s32[1,1,4,2]{2,3,1,0:T(2,128)S(1)}, s32[1,1,4,2]{2,3,1,0:T(2,128)}, u32[]{:S(2)}) copy-start(s32[1,1,4,2]{2,3,1,0:T(2,128)} %param.13) | copy-start | bytes 100
  0.0 30.4 %copy-start.1 = (f32[2,256,256]{2,1,0:T(8,128)S(1)}, f32[2,256,256]{2,1,0:T(8,128)}, u32[]{:S(2)}) copy-start(f32[2,256,256]{2,1,0:T(8,128)} %param.11) | copy-start | bytes 1572868
  0.0 27.1 %collective-permute-start = (f32[4,256,256]{2,1,0:T(8,128)}, f32[4,256,256]{2,1,0:T(8,128)S(1)}, u32[]{:S(2)}, u32[]{:S(2)}) collective-permute-start(f32[4,256,256]{2,1,0:T(8,128)} %param.10), channel_id=1, source_target_pairs={{1,0},{2,1},{3,2},{5,4},{6,5},{7,6},{9,8},{10,9},{11,10},{13,12},{... | collective-permute-start | bytes 3145736 | tf_op jit(solution)/shard_map/ppermute | solution.py:14
  28.3 25.8 %collective-permute-start.1 = (f32[4,256,512]{2,1,0:T(8,128)}, f32[4,256,512]{2,1,0:T(8,128)S(1)}, u32[]{:S(2)}, u32[]{:S(2)}) collective-permute-start(f32[4,256,512]{2,1,0:T(8,128)} %constant_dynamic-update-slice_fusion), channel_id=1, source_target_pairs={{4,0},{8,4},{12,8},{5,1},{9,5},{13,9},{6,2},{10,6},{14,10},{7,3},{... | collective-permute-start | bytes 6291464 | tf_op jit(solution)/shard_map/ppermute | solution.py:14
  77.1 1.2 copy-start.3
  205.2 41.1 %copy-start = (f32[6,512,512]{2,1,0:T(8,128)S(1)}, f32[6,512,512]{2,1,0:T(8,128)}, u32[]{:S(2)}) copy-start(f32[6,512,512]{2,1,0:T(8,128)} %get-tuple-element.344) | copy-start | bytes 18874372
  207.5 38.7 %collective-permute-start.2 = (f32[6,256,512]{2,1,0:T(8,128)S(1)}, f32[6,256,512]{2,1,0:T(8,128)S(1)}, u32[]{:S(2)}, u32[]{:S(2)}) collective-permute-start(f32[6,256,512]{2,1,0:T(8,128)S(1)} %slice.137), channel_id=1, source_target_pairs={{0,4},{4,8},{8,12},{1,5},{5,9},{9,13},{2,6},{6,10},{10,14},{3,7},{... | collective-permute-start | bytes 9437192 | tf_op jit(solution)/shard_map/ppermute | solution.py:14
  247.2 336.9 %copy-start.2 = (f32[4,256,256]{2,1,0:T(8,128)S(1)}, f32[4,256,256]{2,1,0:T(8,128)}, u32[]{:S(2)}) copy-start(f32[4,256,256]{2,1,0:T(8,128)} %param.10) | copy-start | bytes 3145732
  247.2 336.6 %collective-permute-start.3 = (f32[6,256,256]{2,1,0:T(8,128)S(1)}, f32[6,256,256]{2,1,0:T(8,128)S(1)}, u32[]{:S(2)}, u32[]{:S(2)}) collective-permute-start(f32[6,256,256]{2,1,0:T(8,128)S(1)} %slice.175), channel_id=1, source_target_pairs={{0,1},{1,2},{2,3},{4,5},{5,6},{6,7},{8,9},{9,10},{10,11},{12,13},{... | collective-permute-start | bytes 4718600 | tf_op jit(solution)/shard_map/ppermute | solution.py:14
where the time goes:
time: 594 us; the launch traced here: 586 us
  starting transfers between devices  325 us (55%)
  waiting for transfers between devices  98.6 us (17%)
  matrix products  75.6 us (13%)
  local copies, waits for them, and re-layouts  58.1 us (10%)
  other arithmetic  16 us (3%)
  loops' own time  11.8 us (2%)
    ppermute x4, starting transfers between devices, from_behind(): return lax.ppermute(block, axis, route)  325 us
    ppermute x4, waiting for transfers between devices, from_behind(): return lax.ppermute(block, axis, route)  98.6 us
    dot_general x48, matrix products, product(): jnp.dot(left_mat, right_mat, precision=HIGH, preferred_element_type=jnp.f...  75.6 us
    gather x12, local copies, waits for them, and re-layouts  19 us
    dynamic_update_slice x1, local copies, waits for them, and re-layouts, deposit(): lax.dynamic_update_slice(totals, current + contrib, (zero_index, where_yx...  17.2 us
  transfers between devices with their start and end apart: 4, of which 4 were waited for; matrix products, arithmetic and copies ran while one was open for 1% of the time, Pallas kernels for 0%

commit v1 on v0

v1 whole, which is shorter than its diff:
```python
import math

import jax
import jax.numpy as jnp
import numpy as np
from jax import lax
from jax.experimental import pallas as pl
from jax.experimental.pallas import tpu as pltpu
from jax.sharding import PartitionSpec as P

F32 = jnp.float32
BF16 = jnp.bfloat16


def from_behind(block, axis, distance):
    devices = range(lax.axis_size(axis))
    route = [(i - distance, i) for i in devices if i - distance in devices]
    return lax.ppermute(block, axis, route)


def split_tables(width):
    index = np.arange(width)[:, None] * np.arange(width)[None, :] % width
    angles = index * (2.0 * math.pi / width)
    scale = 1.0 / math.sqrt(width)
    cos_table = (np.cos(angles) * scale).astype(np.float32)
    sin_table = (-np.sin(angles) * scale).astype(np.float32)

    def parts(table):
        high = table.astype(BF16)
        low = (table - high.astype(np.float32)).astype(BF16)
        return high, high, low

    left = np.concatenate(
        [
            np.concatenate([*parts(cos_table), *parts(-sin_table)], axis=1),
            np.concatenate([*parts(sin_table), *parts(cos_table)], axis=1),
        ],
        axis=0,
    )
    return jnp.asarray(left), jnp.asarray(np.ascontiguousarray(left.T))


def split(value):
    high = value.astype(BF16)
    low = (value - high.astype(F32)).astype(BF16)
    return high, low


def forward(parts_r, parts_i, left_ref, right_ref):
    width = parts_r[0].shape[0]
    columns = []
    for real, imag in zip(parts_r, parts_i):
        high_r, low_r = split(real)
        high_i, low_i = split(imag)
        columns.append(jnp.concatenate([high_r, low_r, high_r, high_i, low_i, high_i], axis=0))
    data = jnp.concatenate(columns, axis=1)
    half = jnp.dot(left_ref[...], data, preferred_element_type=F32)
    rows = []
    for at in range(len(parts_r)):
        cut = slice(at * width, (at + 1) * width)
        high_r, low_r = split(half[:width, cut])
        high_i, low_i = split(half[width:, cut])
        rows.append(jnp.concatenate([high_r, low_r, high_r, high_i, low_i, high_i], axis=1))
    data = jnp.concatenate(rows, axis=0)
    whole = jnp.dot(data, right_ref[...], preferred_element_type=F32)
    out_r = [whole[at * width : (at + 1) * width, :width] for at in range(len(parts_r))]
    out_i = [whole[at * width : (at + 1) * width, width:] for at in range(len(parts_r))]
    return out_r, out_i


def fill_region(region, own, right, down, diag):
    width = own.shape[-1]
    region[:, :width, :width] = own[...]
    region[:, :width, width:] = right[...]
    region[:, width:, :width] = down[...]
    region[:, width:, width:] = diag[...]


def window(region, plane, top, left):
    width = region.shape[-1] // 2
    base = pl.multiple_of(top // 8 * 8, 8)
    extra = top - base
    rows = region[plane, pl.ds(base, width + 8), :]
    back = jnp.where(left == 0, 0, 2 * width - left)
    rows = pltpu.roll(rows, back, 1)[:, :width]
    up = jnp.where(extra == 0, 0, width + 8 - extra)
    return pltpu.roll(rows, up, 0)[:width]


def deposit(totals, plane, value, top, left):
    width = value.shape[0]
    base = pl.multiple_of(top // 8 * 8, 8)
    tall = jnp.concatenate([value, jnp.zeros((8, width), F32)], axis=0)
    tall = pltpu.roll(tall, top - base, 0)
    wide = pltpu.roll(jnp.concatenate([tall, jnp.zeros_like(tall)], axis=1), left, 1)
    totals[plane, pl.ds(base, width + 8), :] += wide


def write_quarters(totals, upper_left, upper_right, lower_left, lower_right):
    width = upper_left.shape[-1]
    upper_left[...] = totals[:, :width, :width]
    upper_right[...] = totals[:, :width, width:]
    lower_left[...] = totals[:, width:, :width]
    lower_right[...] = totals[:, width:, width:]


def norm_kernel(coords, live, probe, *refs):
    *quarters, totals = refs
    totals[...] = jnp.zeros_like(totals)

    @pl.loop(0, live[0])
    def _(slot):
        power = probe[0] * probe[0] + probe[1] * probe[1]
        deposit(totals, 0, power, coords[slot, 0], coords[slot, 1])

    write_quarters(totals, *quarters)


def wave_kernel(group, coords, own, right, down, diag, probe, phase, left_t, right_t, wave, region):
    fill_region(region, own, right, down, diag)

    @pl.loop(0, coords.shape[0] // group)
    def _(step):
        in_r, in_i = [], []
        for at in range(group):
            slot = step * group + at
            top, left = coords[slot, 0], coords[slot, 1]
            first_r, first_i = window(region, 0, top, left), window(region, 1, top, left)
            in_r.append(probe[0] * first_r - probe[1] * first_i)
            in_i.append(probe[0] * first_i + probe[1] * first_r)
        spec_r, spec_i = forward(in_r, in_i, left_t, right_t)
        moved_r = [a * phase[0] - b * phase[1] for a, b in zip(spec_r, spec_i)]
        minus_i = [-(a * phase[1] + b * phase[0]) for a, b in zip(spec_r, spec_i)]
        wave_r, wave_i = forward(moved_r, minus_i, left_t, right_t)
        for at in range(group):
            wave[step * group + at, 0] = wave_r[at]
            wave[step * group + at, 1] = -wave_i[at]


def back_kernel(
    group, coords, live, wave, own, right, down, diag, amplitude, left_t, right_t, inner, *refs
):
    *quarters, region, totals = refs
    fill_region(region, own, right, down, diag)
    totals[...] = jnp.zeros_like(totals)

    @pl.loop(0, coords.shape[0] // group)
    def _(step):
        in_r, in_i = [], []
        for at in range(group):
            slot = step * group + at
            top, left = coords[slot, 0], coords[slot, 1]
            second_r, second_i = window(region, 0, top, left), window(region, 1, top, left)
            inner[slot, 0] = second_r
            inner[slot, 1] = second_i
            wave_r, wave_i = wave[slot, 0], wave[slot, 1]
            in_r.append(wave_r * second_r - wave_i * second_i)
            in_i.append(wave_r * second_i + wave_i * second_r)
        far_r, far_i = forward(in_r, in_i, left_t, right_t)
        ratio = [
            amplitude[step * group + at]
            * jnp.minimum(lax.rsqrt(far_r[at] * far_r[at] + far_i[at] * far_i[at]), 2.0)
            - 1.0
            for at in range(group)
        ]
        back_r, minus_i = forward(
            [a * b for a, b in zip(far_r, ratio)],
            [-a * b for a, b in zip(far_i, ratio)],
            left_t,
            right_t,
        )
        for at in range(group):
            slot = step * group + at
            top, left = coords[slot, 0], coords[slot, 1]
            real, imag = back_r[at], -minus_i[at]
            second_r, second_i = inner[slot, 0], inner[slot, 1]
            inner[slot, 0] = second_r * real + second_i * imag
            inner[slot, 1] = second_r * imag - second_i * real

            @pl.when(slot < live[0])
            def _():
                wave_r, wave_i = wave[slot, 0], wave[slot, 1]
                deposit(totals, 0, wave_r * real + wave_i * imag, top, left)
                deposit(totals, 1, wave_r * imag - wave_i * real, top, left)
                deposit(totals, 2, wave_r * wave_r + wave_i * wave_i, top, left)

    write_quarters(totals, *quarters)


def grad_kernel(group, coords, live, inner, probe, phase, left_t, right_t, *refs):
    *quarters, totals = refs
    totals[...] = jnp.zeros_like(totals)

    @pl.loop(0, coords.shape[0] // group)
    def _(step):
        in_r = [inner[step * group + at, 0] for at in range(group)]
        in_i = [inner[step * group + at, 1] for at in range(group)]
        turn_r, turn_i = forward(in_r, in_i, left_t, right_t)
        undo_r = [a * phase[0] + b * phase[1] for a, b in zip(turn_r, turn_i)]
        minus_i = [a * phase[1] - b * phase[0] for a, b in zip(turn_r, turn_i)]
        prior_r, minus_p = forward(undo_r, minus_i, left_t, right_t)
        for at in range(group):
            slot = step * group + at
            top, left = coords[slot, 0], coords[slot, 1]
            real, imag = prior_r[at], -minus_p[at]

            @pl.when(slot < live[0])
            def _():
                deposit(totals, 0, probe[0] * real + probe[1] * imag, top, left)
                deposit(totals, 1, probe[0] * imag - probe[1] * real, top, left)

    write_quarters(totals, *quarters)


def settle(quarters):
    upper_left, upper_right, lower_left, lower_right = quarters
    upper_right = upper_right + from_behind(lower_right, "ty", 1)
    from_above = from_behind(lower_left, "ty", 1)
    from_left = from_behind(upper_right, "tx", 1)
    return upper_left + from_above + from_left


def on_device(object_planes, probe, phase, coords, live, amplitude):
    width = probe.shape[-1]
    slots = coords.shape[2]
    group = 2 if slots % 2 == 0 else 1
    left_t, right_t = split_tables(width)
    phase_ri = jnp.stack([jnp.cos(phase), jnp.sin(phase)])
    where_yx = coords[0, 0]
    count = live[0]
    smem = pl.BlockSpec(memory_space=pltpu.SMEM)
    vmem = pl.BlockSpec(memory_space=pltpu.VMEM)

    def plane(*lead):
        return jax.ShapeDtypeStruct((*lead, width, width), F32)

    def scratch(planes):
        return pltpu.VMEM((planes, 2 * width, 2 * width), F32)

    dots = 2 * slots * 2 * 2 * width * 2 * width * 6 * width

    def call(body, n_smem, n_vmem, outs, scratches, flops, name):
        return pl.pallas_call(
            body,
            out_shape=outs,
            in_specs=[smem] * n_smem + [vmem] * n_vmem,
            out_specs=jax.tree.map(lambda _: vmem, outs),
            scratch_shapes=scratches,
            compiler_params=pltpu.CompilerParams(vmem_limit_bytes=48 << 20),
            cost_estimate=pl.CostEstimate(
                flops=flops, bytes_accessed=8 << 20, transcendentals=0
            ),
            name=name,
        )

    def quads(tile):
        right = from_behind(tile, "tx", -1)
        down = from_behind(tile, "ty", -1)
        return tile, right, down, from_behind(right, "ty", -1)

    first, second = object_planes[0:2], object_planes[2:4]
    first_quads = quads(first)
    second_quads = quads(second)

    norm = call(norm_kernel, 2, 1, [plane(1)] * 4, [scratch(1)], 1 << 20, "norm")(
        where_yx, count, probe
    )
    norm_sum = settle(norm)

    def bind(body):
        def bound(*refs):
            body(group, *refs)

        return bound

    wave = call(bind(wave_kernel), 1, 8, plane(slots, 2), [scratch(2)], dots, "wave")(
        where_yx, *first_quads, probe, phase_ri, left_t, right_t
    )
    inner, *second_sums = call(
        bind(back_kernel),
        2,
        8,
        [plane(slots, 2)] + [plane(3)] * 4,
        [scratch(2), scratch(3)],
        dots,
        "back",
    )(where_yx, count, wave, *second_quads, amplitude[0, 0], left_t, right_t)
    first_sums = call(bind(grad_kernel), 2, 5, [plane(2)] * 4, [scratch(2)], dots, "grad")(
        where_yx, count, inner, probe, phase_ri, left_t, right_t
    )
    second_sum = settle(second_sums)
    first_sum = settle(first_sums)
    new_first = first + first_sum / (norm_sum + 1.0)
    new_second = second + second_sum[0:2] / (second_sum[2:3] + 1.0)
    return jnp.concatenate([new_first, new_second])


def solution(mesh):
    return jax.shard_map(
        on_device,
        mesh=mesh,
        in_specs=(
            P(None, ("groups", "ty"), "tx"),
            P(),
            P(),
            P(("groups", "ty"), "tx", None, None),
            P(("groups", "ty"), "tx"),
            P(("groups", "ty"), "tx", None, None, None),
        ),
        out_specs=P(None, ("groups", "ty"), "tx"),
        check_vma=False,
    )
```

time: 594 us -> 122 us (0.21)
  the two profiles are of different devices: /device:TPU:22 before, /device:TPU:0 now
where the time goes in v1:
time: 122 us
  starting transfers between devices  41.1 us (34%)
  Pallas kernels  38 us (31%)
  waiting for transfers between devices  36.5 us (30%)
  local copies, waits for them, and re-layouts  3.83 us (3%)
  other arithmetic  1.75 us (1%)
    ppermute x15, starting transfers between devices, from_behind(): return lax.ppermute(block, axis, route)  41.1 us
    ppermute x15, waiting for transfers between devices, from_behind(): return lax.ppermute(block, axis, route)  36.5 us
    pallas_call x1, Pallas kernels, on_device(): call(bind(back_kernel), 2, 8, [plane(slots, 2)] + [plane(3)] * 4, [scratc...  14.3 us
    pallas_call x1, Pallas kernels, on_device(): call(bind(wave_kernel), 1, 8, plane(slots, 2), [scratch(2)], dots, 'wave')  12.6 us
    pallas_call x1, Pallas kernels, on_device(): call(bind(grad_kernel), 2, 5, [plane(2)] * 4, [scratch(2)], dots, 'grad')  10.1 us
  transfers between devices with their start and end apart: 15, of which 4 were waited for; matrix products, arithmetic and copies ran while one was open for 1% of the time, Pallas kernels for 19%

profile of v1, /device:TPU:0, one launch (start us, length us, event | category | flops | bytes accessed | tf_op | source)
XLA Modules:
  0.0 122.2 jit_solution(7233876563287329422)
XLA Ops:
  0.0 1.3 %fusion.2 = (f32[2,256,256]{2,1,0:T(8,128)S(1)}, f32[2,256,256]{2,1,0:T(8,128)S(1)}) fusion(f32[4,256,256]{2,1,0:T(8,128)} %param.8), kind=kLoop, calls=%fused_computation.11 | loop fusion | bytes 2097152 | tf_op jit(solution)/shard_map/slice | solution.py:261
  1.4 1.3 %collective-permute-start = (f32[2,256,256]{2,1,0:T(8,128)S(1)}, f32[2,256,256]{2,1,0:T(8,128)S(1)}, u32[]{:S(2)}, u32[]{:S(2)}) collective-permute-start(f32[2,256,256]{2,1,0:T(8,128)S(1)} %get-tuple-element.34.refs_1_), channel_id=1, source_target_pairs={{1,0},{2,1},{3,2},{5,4},{6,5},{7,6},{9,8},{10,9},{11,10},{13,12},{... | collective-permute-start | bytes 1572872 | tf_op jit(solution)/shard_map/ppermute | solution.py:18
  2.7 1.3 %collective-permute-start.3 = (f32[2,256,256]{2,1,0:T(8,128)S(1)}, f32[2,256,256]{2,1,0:T(8,128)S(1)}, u32[]{:S(2)}, u32[]{:S(2)}) collective-permute-start(f32[2,256,256]{2,1,0:T(8,128)S(1)} %get-tuple-element.33.refs_3_), channel_id=1, source_target_pairs={{1,0},{2,1},{3,2},{5,4},{6,5},{7,6},{9,8},{10,9},{11,10},{13,12},{... | collective-permute-start | bytes 1572872 | tf_op jit(solution)/shard_map/ppermute | solution.py:18
  4.0 1.3 %collective-permute-start.1 = (f32[2,256,256]{2,1,0:T(8,128)S(1)}, f32[2,256,256]{2,1,0:T(8,128)}, u32[]{:S(2)}, u32[]{:S(2)}) collective-permute-start(f32[2,256,256]{2,1,0:T(8,128)S(1)} %get-tuple-element.34.refs_1_), channel_id=1, source_target_pairs={{4,0},{8,4},{12,8},{5,1},{9,5},{13,9},{6,2},{10,6},{14,10},{7,3},{... | collective-permute-start | bytes 1572872 | tf_op jit(solution)/shard_map/ppermute | solution.py:18
  5.3 13.8 %collective-permute-done.refs_2_ = f32[2,256,256]{2,1,0:T(8,128)S(1)} collective-permute-done((f32[2,256,256]{2,1,0:T(8,128)S(1)}, f32[2,256,256]{2,1,0:T(8,128)S(1)}, u32[]{:S(2)}, u32[]{:S(2)}) %collective-permute-start) | collective-permute-done | bytes 524320 | tf_op jit(solution)/shard_map/ppermute | solution.py:18
  19.0 1.3 %collective-permute-start.2 = (f32[2,256,256]{2,1,0:T(8,128)S(1)}, f32[2,256,256]{2,1,0:T(8,128)}, u32[]{:S(2)}, u32[]{:S(2)}) collective-permute-start(f32[2,256,256]{2,1,0:T(8,128)S(1)} %collective-permute-done.refs_2_), channel_id=1, source_target_pairs={{4,0},{8,4},{12,8},{5,1},{9,5},{13,9},{6,2},{10,6},{14,10},{7,3},{... | collective-permute-start | bytes 1572872 | tf_op jit(solution)/shard_map/ppermute | solution.py:18
  20.3 1.3 %collective-permute-start.4 = (f32[2,256,256]{2,1,0:T(8,128)S(1)}, f32[2,256,256]{2,1,0:T(8,128)S(1)}, u32[]{:S(2)}, u32[]{:S(2)}) collective-permute-start(f32[2,256,256]{2,1,0:T(8,128)S(1)} %get-tuple-element.33.refs_3_), channel_id=1, source_target_pairs={{4,0},{8,4},{12,8},{5,1},{9,5},{13,9},{6,2},{10,6},{14,10},{7,3},{... | collective-permute-start | bytes 1572872 | tf_op jit(solution)/shard_map/ppermute | solution.py:18
  21.6 0.0 copy-done.5
  21.6 0.1 copy.11.refs_0_.coords
  22.4 1.0 cosine_bitcast_fusion
  23.4 6.0 %collective-permute-done.3.refs_4_ = f32[2,256,256]{2,1,0:T(8,128)S(1)} collective-permute-done((f32[2,256,256]{2,1,0:T(8,128)S(1)}, f32[2,256,256]{2,1,0:T(8,128)S(1)}, u32[]{:S(2)}, u32[]{:S(2)}) %collective-permute-start.3) | collective-permute-done | bytes 524320 | tf_op jit(solution)/shard_map/ppermute | solution.py:18
  29.5 1.3 %collective-permute-start.5 = (f32[2,256,256]{2,1,0:T(8,128)S(1)}, f32[2,256,256]{2,1,0:T(8,128)S(1)}, u32[]{:S(2)}, u32[]{:S(2)}) collective-permute-start(f32[2,256,256]{2,1,0:T(8,128)S(1)} %collective-permute-done.3.refs_4_), channel_id=1, source_target_pairs={{4,0},{8,4},{12,8},{5,1},{9,5},{13,9},{6,2},{10,6},{14,10},{7,3},{... | collective-permute-start | bytes 1572872 | tf_op jit(solution)/shard_map/ppermute | solution.py:18
  30.7 0.0 collective-permute-done.1.refs_3_
  30.8 0.0 collective-permute-done.2.refs_4_
  30.8 0.0 copy-start.1
  30.8 1.4 %copy-done.1 = bf16[512,1536]{1,0:T(8,128)(2,1)S(1)} copy-done((bf16[512,1536]{1,0:T(8,128)(2,1)S(1)}, bf16[512,1536]{1,0:T(8,128)(2,1)}, u32[]{:S(2)}) %copy-start.1) | copy-done | bytes 1572888
  32.2 12.6 %wave.1.refs_2_ = f32[4,2,256,256]{3,2,1,0:T(8,128)} custom-call(s32[4,2]{1,0:T(4,128)S(1)} %copy.11.refs_0_.coords, f32[2,256,256]{2,1,0:T(8,128)S(1)} %get-tuple-element.34.refs_1_, f32[2,256,256]{2,1,0:T(8,128)S(1)} %collective-permute-done.refs_2_, f32[2,256,256]{2,1,0:T(8,128)} %collective-permute-done.1.refs_3_, ...), custom_call_target="tpu_custom_call" | custom-call | flops 6442450944 | bytes 8388608 | tf_op jit(solution)/shard_map/wave/pallas_call | solution.py:276
  44.8 0.0 collective-permute-done.4.refs_5_
  44.8 0.0 collective-permute-done.5.refs_6_
  44.8 14.3 %back.1 = (f32[4,2,256,256]{3,2,1,0:T(8,128)}, f32[3,256,256]{2,1,0:T(8,128)S(1)}, f32[3,256,256]{2,1,0:T(8,128)S(1)}, f32[3,256,256]{2,1,0:T(8,128)S(1)}, f32[3,256,256]{2,1,0:T(8,128)S(1)}) custom-call(s32[4,2]{1,0:T(4,128)S(1)} %copy.11.refs_0_.coords, s32[1]{0:T(128)} %bitcast.11.refs_1_, f32[4,2,256,256]{3,2,1,0:T(8,128)} %wave.1.refs_2_, ...), custom_call_target="tpu_custom_call" | custom-call | flops 6442450944 | bytes 8388608 | tf_op jit(solution)/shard_map/back/pallas_call | solution.py:279
  59.1 2.6 %collective-permute-start.13 = (f32[3,256,256]{2,1,0:T(8,128)S(1)}, f32[3,256,256]{2,1,0:T(8,128)S(1)}, u32[]{:S(2)}, u32[]{:S(2)}) collective-permute-start(f32[3,256,256]{2,1,0:T(8,128)S(1)} %get-tuple-element.30), channel_id=1, source_target_pairs={{0,4},{4,8},{8,12},{1,5},{5,9},{9,13},{2,6},{6,10},{10,14},{3,7},{... | collective-permute-start | bytes 2359304 | tf_op jit(solution)/shard_map/ppermute | solution.py:18
  61.7 1.0 norm.1
  62.7 5.4 %collective-permute-start.10 = (f32[1,256,256]{2,1,0:T(8,128)S(1)}, f32[1,256,256]{2,1,0:T(8,128)S(1)}, u32[]{:S(2)}, u32[]{:S(2)}) collective-permute-start(f32[1,256,256]{2,1,0:T(8,128)S(1)} %get-tuple-element.26), channel_id=1, source_target_pairs={{0,4},{4,8},{8,12},{1,5},{5,9},{9,13},{2,6},{6,10},{10,14},{3,7},{... | collective-permute-start | bytes 786440 | tf_op jit(solution)/shard_map/ppermute | solution.py:18
  68.1 3.2 %collective-permute-start.12 = (f32[3,256,256]{2,1,0:T(8,128)S(1)}, f32[3,256,256]{2,1,0:T(8,128)S(1)}, u32[]{:S(2)}, u32[]{:S(2)}) collective-permute-start(f32[3,256,256]{2,1,0:T(8,128)S(1)} %get-tuple-element.28), channel_id=1, source_target_pairs={{0,4},{4,8},{8,12},{1,5},{5,9},{9,13},{2,6},{6,10},{10,14},{3,7},{... | collective-permute-start | bytes 2359304 | tf_op jit(solution)/shard_map/ppermute | solution.py:18
  71.3 0.0 collective-permute-done.13
  71.3 0.1 add.48
  71.4 3.7 %collective-permute-start.14 = (f32[3,256,256]{2,1,0:T(8,128)S(1)}, f32[3,256,256]{2,1,0:T(8,128)S(1)}, u32[]{:S(2)}, u32[]{:S(2)}) collective-permute-start(f32[3,256,256]{2,1,0:T(8,128)S(1)} %add.48), channel_id=1, source_target_pairs={{0,1},{1,2},{2,3},{4,5},{5,6},{6,7},{8,9},{9,10},{10,11},{12,13},{... | collective-permute-start | bytes 2359304 | tf_op jit(solution)/shard_map/ppermute | solution.py:18
  75.2 0.0 copy-done.2
  75.2 10.1 %grad.1 = (f32[2,256,256]{2,1,0:T(8,128)S(1)}, f32[2,256,256]{2,1,0:T(8,128)S(1)}, f32[2,256,256]{2,1,0:T(8,128)S(1)}, f32[2,256,256]{2,1,0:T(8,128)S(1)}) custom-call(s32[4,2]{1,0:T(4,128)S(1)} %copy.11.refs_0_.coords, s32[1]{0:T(128)} %bitcast.12.refs_1_, f32[4,2,256,256]{3,2,1,0:T(8,128)} %get-tuple-element.18.refs_2_, f32[2,256,256]{2,1,0:T(8,128)S(1)} %copy-done, ...), custom_call_target="tpu_custom_call" | custom-call | flops 6442450944 | bytes 8388608 | tf_op jit(solution)/shard_map/grad/pallas_call | solution.py:288
  85.2 4.3 %collective-permute-start.7 = (f32[2,256,256]{2,1,0:T(8,128)S(1)}, f32[2,256,256]{2,1,0:T(8,128)S(1)}, u32[]{:S(2)}, u32[]{:S(2)}) collective-permute-start(f32[2,256,256]{2,1,0:T(8,128)S(1)} %get-tuple-element.22), channel_id=1, source_target_pairs={{0,4},{4,8},{8,12},{1,5},{5,9},{9,13},{2,6},{6,10},{10,14},{3,7},{... | collective-permute-start | bytes 1572872 | tf_op jit(solution)/shard_map/ppermute | solution.py:18
  89.5 6.5 %collective-permute-start.9 = (f32[1,256,256]{2,1,0:T(8,128)S(1)}, f32[1,256,256]{2,1,0:T(8,128)S(1)}, u32[]{:S(2)}, u32[]{:S(2)}) collective-permute-start(f32[1,256,256]{2,1,0:T(8,128)S(1)} %get-tuple-element.24), channel_id=1, source_target_pairs={{0,4},{4,8},{8,12},{1,5},{5,9},{9,13},{2,6},{6,10},{10,14},{3,7},{... | collective-permute-start | bytes 786440 | tf_op jit(solution)/shard_map/ppermute | solution.py:18
  96.0 0.0 collective-permute-done.10
  96.1 1.9 %collective-permute-start.11 = (f32[1,256,256]{2,1,0:T(8,128)S(1)}, f32[1,256,256]{2,1,0:T(8,128)S(1)}, u32[]{:S(2)}, u32[]{:S(2)}) collective-permute-start(f32[1,256,256]{2,1,0:T(8,128)S(1)} %add.43), channel_id=1, source_target_pairs={{0,1},{1,2},{2,3},{4,5},{5,6},{6,7},{8,9},{9,10},{10,11},{12,13},{... | collective-permute-start | bytes 786440 | tf_op jit(solution)/shard_map/ppermute | solution.py:18
  98.0 0.0 collective-permute-done.9
  98.0 5.7 %collective-permute-done.11 = f32[1,256,256]{2,1,0:T(8,128)S(1)} collective-permute-done((f32[1,256,256]{2,1,0:T(8,128)S(1)}, f32[1,256,256]{2,1,0:T(8,128)S(1)}, u32[]{:S(2)}, u32[]{:S(2)}) %collective-permute-start.11) | collective-permute-done | bytes 262176 | tf_op jit(solution)/shard_map/ppermute | solution.py:18
  103.7 0.1 add_bitcast_fusion
  103.7 1.3 %collective-permute-start.6 = (f32[2,256,256]{2,1,0:T(8,128)S(1)}, f32[2,256,256]{2,1,0:T(8,128)S(1)}, u32[]{:S(2)}, u32[]{:S(2)}) collective-permute-start(f32[2,256,256]{2,1,0:T(8,128)S(1)} %get-tuple-element.20), channel_id=1, source_target_pairs={{0,4},{4,8},{8,12},{1,5},{5,9},{9,13},{2,6},{6,10},{10,14},{3,7},{... | collective-permute-start | bytes 1572872 | tf_op jit(solution)/shard_map/ppermute | solution.py:18
  105.0 0.0 collective-permute-done.7
  105.0 0.1 add.40
  105.1 0.0 copy-start.3
  105.1 4.5 %collective-permute-start.8 = (f32[2,256,256]{2,1,0:T(8,128)S(1)}, f32[2,256,256]{2,1,0:T(8,128)S(1)}, u32[]{:S(2)}, u32[]{:S(2)}) collective-permute-start(f32[2,256,256]{2,1,0:T(8,128)S(1)} %add.40), channel_id=1, source_target_pairs={{0,1},{1,2},{2,3},{4,5},{5,6},{6,7},{8,9},{9,10},{10,11},{12,13},{... | collective-permute-start | bytes 1572872 | tf_op jit(solution)/shard_map/ppermute | solution.py:18
  109.7 0.0 collective-permute-done.12
  109.7 0.0 collective-permute-done.14
  109.7 0.2 add_add_fusion
  109.9 0.0 collective-permute-done.6
  109.9 11.0 %collective-permute-done.8 = f32[2,256,256]{2,1,0:T(8,128)S(1)} collective-permute-done((f32[2,256,256]{2,1,0:T(8,128)S(1)}, f32[2,256,256]{2,1,0:T(8,128)S(1)}, u32[]{:S(2)}, u32[]{:S(2)}) %collective-permute-start.8) | collective-permute-done | bytes 524320 | tf_op jit(solution)/shard_map/ppermute | solution.py:18
  120.9 0.2 divide_add_fusion
  121.1 1.0 pad_maximum_fusion
  (10 shorter events, 0.1 us)
Async XLA Ops:
  0.0 21.6 %copy-start.5 = (s32[1,1,4,2]{2,3,1,0:T(2,128)S(1)}, s32[1,1,4,2]{2,3,1,0:T(2,128)}, u32[]{:S(2)}) copy-start(s32[1,1,4,2]{2,3,1,0:T(2,128)} %param.11) | copy-start | bytes 100
  0.0 22.4 %copy-start.4 = (f32[256,256]{1,0:T(8,128)S(1)}, f32[256,256]{1,0:T(8,128)}, u32[]{:S(2)}) copy-start(f32[256,256]{1,0:T(8,128)} %param.10) | copy-start | bytes 786436
  0.0 30.8 %copy-start = (f32[2,256,256]{2,1,0:T(8,128)S(1)}, f32[2,256,256]{2,1,0:T(8,128)}, u32[]{:S(2)}) copy-start(f32[2,256,256]{2,1,0:T(8,128)} %probe.1) | copy-start | bytes 1572868
  1.4 17.7 %collective-permute-start = (f32[2,256,256]{2,1,0:T(8,128)S(1)}, f32[2,256,256]{2,1,0:T(8,128)S(1)}, u32[]{:S(2)}, u32[]{:S(2)}) collective-permute-start(f32[2,256,256]{2,1,0:T(8,128)S(1)} %get-tuple-element.34.refs_1_), channel_id=1, source_target_pairs={{1,0},{2,1},{3,2},{5,4},{6,5},{7,6},{9,8},{10,9},{11,10},{13,12},{... | collective-permute-start | bytes 1572872 | tf_op jit(solution)/shard_map/ppermute | solution.py:18
  2.7 26.8 %collective-permute-start.3 = (f32[2,256,256]{2,1,0:T(8,128)S(1)}, f32[2,256,256]{2,1,0:T(8,128)S(1)}, u32[]{:S(2)}, u32[]{:S(2)}) collective-permute-start(f32[2,256,256]{2,1,0:T(8,128)S(1)} %get-tuple-element.33.refs_3_), channel_id=1, source_target_pairs={{1,0},{2,1},{3,2},{5,4},{6,5},{7,6},{9,8},{10,9},{11,10},{13,12},{... | collective-permute-start | bytes 1572872 | tf_op jit(solution)/shard_map/ppermute | solution.py:18
  4.0 26.8 %collective-permute-start.1 = (f32[2,256,256]{2,1,0:T(8,128)S(1)}, f32[2,256,256]{2,1,0:T(8,128)}, u32[]{:S(2)}, u32[]{:S(2)}) collective-permute-start(f32[2,256,256]{2,1,0:T(8,128)S(1)} %get-tuple-element.34.refs_1_), channel_id=1, source_target_pairs={{4,0},{8,4},{12,8},{5,1},{9,5},{13,9},{6,2},{10,6},{14,10},{7,3},{... | collective-permute-start | bytes 1572872 | tf_op jit(solution)/shard_map/ppermute | solution.py:18
  19.0 11.7 %collective-permute-start.2 = (f32[2,256,256]{2,1,0:T(8,128)S(1)}, f32[2,256,256]{2,1,0:T(8,128)}, u32[]{:S(2)}, u32[]{:S(2)}) collective-permute-start(f32[2,256,256]{2,1,0:T(8,128)S(1)} %collective-permute-done.refs_2_), channel_id=1, source_target_pairs={{4,0},{8,4},{12,8},{5,1},{9,5},{13,9},{6,2},{10,6},{14,10},{7,3},{... | collective-permute-start | bytes 1572872 | tf_op jit(solution)/shard_map/ppermute | solution.py:18
  20.3 24.4 %collective-permute-start.4 = (f32[2,256,256]{2,1,0:T(8,128)S(1)}, f32[2,256,256]{2,1,0:T(8,128)S(1)}, u32[]{:S(2)}, u32[]{:S(2)}) collective-permute-start(f32[2,256,256]{2,1,0:T(8,128)S(1)} %get-tuple-element.33.refs_3_), channel_id=1, source_target_pairs={{4,0},{8,4},{12,8},{5,1},{9,5},{13,9},{6,2},{10,6},{14,10},{7,3},{... | collective-permute-start | bytes 1572872 | tf_op jit(solution)/shard_map/ppermute | solution.py:18
  29.5 15.3 %collective-permute-start.5 = (f32[2,256,256]{2,1,0:T(8,128)S(1)}, f32[2,256,256]{2,1,0:T(8,128)S(1)}, u32[]{:S(2)}, u32[]{:S(2)}) collective-permute-start(f32[2,256,256]{2,1,0:T(8,128)S(1)} %collective-permute-done.3.refs_4_), channel_id=1, source_target_pairs={{4,0},{8,4},{12,8},{5,1},{9,5},{13,9},{6,2},{10,6},{14,10},{7,3},{... | collective-permute-start | bytes 1572872 | tf_op jit(solution)/shard_map/ppermute | solution.py:18
  30.8 1.4 %copy-start.1 = (bf16[512,1536]{1,0:T(8,128)(2,1)S(1)}, bf16[512,1536]{1,0:T(8,128)(2,1)}, u32[]{:S(2)}) copy-start(bf16[512,1536]{1,0:T(8,128)(2,1)} %constant.6.clone.refs_7_.refs_8_.refs_5_) | copy-start | bytes 4718596
  59.1 16.0 %copy-start.2 = (bf16[512,1536]{1,0:T(8,128)(2,1)S(1)}, bf16[512,1536]{1,0:T(8,128)(2,1)}, u32[]{:S(2)}) copy-start(bf16[512,1536]{1,0:T(8,128)(2,1)} %constant.6.clone.refs_7_.refs_8_.refs_5_) | copy-start | bytes 4718596
  59.1 12.2 %collective-permute-start.13 = (f32[3,256,256]{2,1,0:T(8,128)S(1)}, f32[3,256,256]{2,1,0:T(8,128)S(1)}, u32[]{:S(2)}, u32[]{:S(2)}) collective-permute-start(f32[3,256,256]{2,1,0:T(8,128)S(1)} %get-tuple-element.30), channel_id=1, source_target_pairs={{0,4},{4,8},{8,12},{1,5},{5,9},{9,13},{2,6},{6,10},{10,14},{3,7},{... | collective-permute-start | bytes 2359304 | tf_op jit(solution)/shard_map/ppermute | solution.py:18
  62.7 33.3 %collective-permute-start.10 = (f32[1,256,256]{2,1,0:T(8,128)S(1)}, f32[1,256,256]{2,1,0:T(8,128)S(1)}, u32[]{:S(2)}, u32[]{:S(2)}) collective-permute-start(f32[1,256,256]{2,1,0:T(8,128)S(1)} %get-tuple-element.26), channel_id=1, source_target_pairs={{0,4},{4,8},{8,12},{1,5},{5,9},{9,13},{2,6},{6,10},{10,14},{3,7},{... | collective-permute-start | bytes 786440 | tf_op jit(solution)/shard_map/ppermute | solution.py:18
  68.1 41.6 %collective-permute-start.12 = (f32[3,256,256]{2,1,0:T(8,128)S(1)}, f32[3,256,256]{2,1,0:T(8,128)S(1)}, u32[]{:S(2)}, u32[]{:S(2)}) collective-permute-start(f32[3,256,256]{2,1,0:T(8,128)S(1)} %get-tuple-element.28), channel_id=1, source_target_pairs={{0,4},{4,8},{8,12},{1,5},{5,9},{9,13},{2,6},{6,10},{10,14},{3,7},{... | collective-permute-start | bytes 2359304 | tf_op jit(solution)/shard_map/ppermute | solution.py:18
  71.4 38.3 %collective-permute-start.14 = (f32[3,256,256]{2,1,0:T(8,128)S(1)}, f32[3,256,256]{2,1,0:T(8,128)S(1)}, u32[]{:S(2)}, u32[]{:S(2)}) collective-permute-start(f32[3,256,256]{2,1,0:T(8,128)S(1)} %add.48), channel_id=1, source_target_pairs={{0,1},{1,2},{2,3},{4,5},{5,6},{6,7},{8,9},{9,10},{10,11},{12,13},{... | collective-permute-start | bytes 2359304 | tf_op jit(solution)/shard_map/ppermute | solution.py:18
  85.2 19.8 %collective-permute-start.7 = (f32[2,256,256]{2,1,0:T(8,128)S(1)}, f32[2,256,256]{2,1,0:T(8,128)S(1)}, u32[]{:S(2)}, u32[]{:S(2)}) collective-permute-start(f32[2,256,256]{2,1,0:T(8,128)S(1)} %get-tuple-element.22), channel_id=1, source_target_pairs={{0,4},{4,8},{8,12},{1,5},{5,9},{9,13},{2,6},{6,10},{10,14},{3,7},{... | collective-permute-start | bytes 1572872 | tf_op jit(solution)/shard_map/ppermute | solution.py:18
  89.5 8.5 %collective-permute-start.9 = (f32[1,256,256]{2,1,0:T(8,128)S(1)}, f32[1,256,256]{2,1,0:T(8,128)S(1)}, u32[]{:S(2)}, u32[]{:S(2)}) collective-permute-start(f32[1,256,256]{2,1,0:T(8,128)S(1)} %get-tuple-element.24), channel_id=1, source_target_pairs={{0,4},{4,8},{8,12},{1,5},{5,9},{9,13},{2,6},{6,10},{10,14},{3,7},{... | collective-permute-start | bytes 786440 | tf_op jit(solution)/shard_map/ppermute | solution.py:18
  96.1 7.6 %collective-permute-start.11 = (f32[1,256,256]{2,1,0:T(8,128)S(1)}, f32[1,256,256]{2,1,0:T(8,128)S(1)}, u32[]{:S(2)}, u32[]{:S(2)}) collective-permute-start(f32[1,256,256]{2,1,0:T(8,128)S(1)} %add.43), channel_id=1, source_target_pairs={{0,1},{1,2},{2,3},{4,5},{5,6},{6,7},{8,9},{9,10},{10,11},{12,13},{... | collective-permute-start | bytes 786440 | tf_op jit(solution)/shard_map/ppermute | solution.py:18
  103.7 6.2 %collective-permute-start.6 = (f32[2,256,256]{2,1,0:T(8,128)S(1)}, f32[2,256,256]{2,1,0:T(8,128)S(1)}, u32[]{:S(2)}, u32[]{:S(2)}) collective-permute-start(f32[2,256,256]{2,1,0:T(8,128)S(1)} %get-tuple-element.20), channel_id=1, source_target_pairs={{0,4},{4,8},{8,12},{1,5},{5,9},{9,13},{2,6},{6,10},{10,14},{3,7},{... | collective-permute-start | bytes 1572872 | tf_op jit(solution)/shard_map/ppermute | solution.py:18
  105.1 15.8 %copy-start.3 = (f32[4,256,256]{2,1,0:T(8,128)S(1)}, f32[4,256,256]{2,1,0:T(8,128)}, u32[]{:S(2)}) copy-start(f32[4,256,256]{2,1,0:T(8,128)} %param.8) | copy-start | bytes 3145732
  105.1 15.8 %collective-permute-start.8 = (f32[2,256,256]{2,1,0:T(8,128)S(1)}, f32[2,256,256]{2,1,0:T(8,128)S(1)}, u32[]{:S(2)}, u32[]{:S(2)}) collective-permute-start(f32[2,256,256]{2,1,0:T(8,128)S(1)} %add.40), channel_id=1, source_target_pairs={{0,1},{1,2},{2,3},{4,5},{5,6},{6,7},{8,9},{9,10},{10,11},{12,13},{... | collective-permute-start | bytes 1572872 | tf_op jit(solution)/shard_map/ppermute | solution.py:18

commit v2 on v1

v2 whole, which is shorter than its diff:
```python
import math

import jax
import jax.numpy as jnp
import numpy as np
from jax import lax
from jax.experimental import pallas as pl
from jax.experimental.pallas import tpu as pltpu
from jax.sharding import PartitionSpec as P

F32 = jnp.float32
BF16 = jnp.bfloat16


def split_tables(width):
    index = np.arange(width)[:, None] * np.arange(width)[None, :] % width
    angles = index * (2.0 * math.pi / width)
    scale = 1.0 / math.sqrt(width)
    cos_table = (np.cos(angles) * scale).astype(np.float32)
    sin_table = (-np.sin(angles) * scale).astype(np.float32)

    def parts(table):
        high = table.astype(BF16)
        low = (table - high.astype(np.float32)).astype(BF16)
        return high, high, low

    left = np.concatenate(
        [
            np.concatenate([*parts(cos_table), *parts(-sin_table)], axis=1),
            np.concatenate([*parts(sin_table), *parts(cos_table)], axis=1),
        ],
        axis=0,
    )
    return jnp.asarray(left), jnp.asarray(np.ascontiguousarray(left.T))


def split(value):
    high = value.astype(BF16)
    low = (value - high.astype(F32)).astype(BF16)
    return high, low


def forward(parts_r, parts_i, left_ref, right_ref):
    width = parts_r[0].shape[0]
    columns = []
    for real, imag in zip(parts_r, parts_i):
        high_r, low_r = split(real)
        high_i, low_i = split(imag)
        columns.append(jnp.concatenate([high_r, low_r, high_r, high_i, low_i, high_i], axis=0))
    data = jnp.concatenate(columns, axis=1)
    half = jnp.dot(left_ref[...], data, preferred_element_type=F32)
    rows = []
    for at in range(len(parts_r)):
        cut = slice(at * width, (at + 1) * width)
        high_r, low_r = split(half[:width, cut])
        high_i, low_i = split(half[width:, cut])
        rows.append(jnp.concatenate([high_r, low_r, high_r, high_i, low_i, high_i], axis=1))
    data = jnp.concatenate(rows, axis=0)
    whole = jnp.dot(data, right_ref[...], preferred_element_type=F32)
    out_r = [whole[at * width : (at + 1) * width, :width] for at in range(len(parts_r))]
    out_i = [whole[at * width : (at + 1) * width, width:] for at in range(len(parts_r))]
    return out_r, out_i


def neighbours():
    row, column = lax.axis_index("ty"), lax.axis_index("tx")
    has = {
        "up": row > 0,
        "down": row < lax.axis_size("ty") - 1,
        "left": column > 0,
        "right": column < lax.axis_size("tx") - 1,
    }
    where = {
        "up": {"ty": row - 1},
        "down": {"ty": row + 1},
        "left": {"tx": column - 1},
        "right": {"tx": column + 1},
    }
    return has, where


def greet(has, where):
    barrier = pltpu.get_barrier_semaphore()
    for side, there in has.items():

        @pl.when(there)
        def _():
            pl.semaphore_signal(
                barrier, inc=1, device_id=where[side], device_id_type=pl.DeviceIdType.MESH
            )

    peers = sum(there.astype(jnp.int32) for there in has.values())
    pl.semaphore_wait(barrier, peers)


class Link:
    def __init__(self, source, target, sems, at, device, sends, receives):
        self.copy = pltpu.make_async_remote_copy(
            src_ref=source,
            dst_ref=target,
            send_sem=sems[0].at[at],
            recv_sem=sems[1].at[at],
            device_id=device,
            device_id_type=pl.DeviceIdType.MESH,
        )
        self.sends, self.receives = sends, receives

    def start(self):
        pl.when(self.sends)(self.copy.start)

    def sent(self):
        pl.when(self.sends)(self.copy.wait_send)

    def arrived(self):
        pl.when(self.receives)(self.copy.wait_recv)


def window(region, plane, top, left):
    width = region.shape[-1] // 2
    base = pl.multiple_of(top // 8 * 8, 8)
    extra = top - base
    rows = region[plane, pl.ds(base, width + 8), :]
    back = jnp.where(left == 0, 0, 2 * width - left)
    rows = pltpu.roll(rows, back, 1)[:, :width]
    up = jnp.where(extra == 0, 0, width + 8 - extra)
    return pltpu.roll(rows, up, 0)[:width]


def deposit(totals, plane, value, top, left):
    width = value.shape[0]
    base = pl.multiple_of(top // 8 * 8, 8)
    tall = jnp.concatenate([value, jnp.zeros((8, width), F32)], axis=0)
    tall = pltpu.roll(tall, top - base, 0)
    wide = pltpu.roll(jnp.concatenate([tall, jnp.zeros_like(tall)], axis=1), left, 1)
    totals[plane, pl.ds(base, width + 8), :] += wide


def write_quarters(totals, upper_left, upper_right, lower_left, lower_right):
    width = upper_left.shape[-1]
    upper_left[...] = totals[:, :width, :width]
    upper_right[...] = totals[:, :width, width:]
    lower_left[...] = totals[:, width:, :width]
    lower_right[...] = totals[:, width:, width:]


class Halo:
    def __init__(self, own, region, sems, at, has, where):
        planes, width = own.shape[0], own.shape[-1]
        upper, lower = slice(0, width), slice(width, 2 * width)
        both = (has["up"] & has["right"], has["down"] & has["right"])
        self.own, self.region, self.has = own, region, has
        self.across, self.down, self.corner = [], [], []
        for plane in range(planes):
            mine = own.at[plane]
            right = region.at[plane, upper, lower]
            below = region.at[plane, lower, upper]
            beyond = region.at[plane, lower, lower]
            sem = at + 3 * plane
            self.across.append(
                Link(mine, right, sems, sem, where["left"], has["left"], has["right"])
            )
            self.down.append(
                Link(mine, below, sems, sem + 1, where["up"], has["up"], has["down"])
            )
            self.corner.append(Link(right, beyond, sems, sem + 2, where["up"], *both))

    def start(self):
        for link in (*self.across, *self.down):
            link.start()

    def blank(self):
        has, region, width = self.has, self.region, self.own.shape[-1]
        upper, lower = slice(0, width), slice(width, 2 * width)
        zeros = jnp.zeros(self.own.shape, F32)
        region[:, upper, upper] = self.own[...]

        @pl.when(jnp.logical_not(has["right"]))
        def _():
            region[:, upper, lower] = zeros

        @pl.when(jnp.logical_not(has["down"]))
        def _():
            region[:, lower, upper] = zeros

        @pl.when(jnp.logical_not(has["down"] & has["right"]))
        def _():
            region[:, lower, lower] = zeros

    def turn(self, plane):
        self.across[plane].arrived()
        self.corner[plane].start()

    def finish(self):
        for link in (*self.down, *self.corner):
            link.arrived()
        for link in (*self.across, *self.down, *self.corner):
            link.sent()


class Sums:
    def __init__(self, quarters, passing, got, sems, at, has, where):
        self.quarters, self.passing, self.got, self.has = quarters, passing, got, has
        _, _, lower_left, lower_right = quarters
        self.corner, self.down, self.across = [], [], []
        for plane in range(passing.shape[0]):
            sem = at + 3 * plane
            below = (where["down"], has["down"], has["up"])
            beside = (where["right"], has["right"], has["left"])
            self.corner.append(
                Link(lower_right.at[plane], got.at[0, plane], sems, sem, *below)
            )
            self.down.append(
                Link(lower_left.at[plane], got.at[1, plane], sems, sem + 1, *below)
            )
            self.across.append(Link(passing.at[plane], got.at[2, plane], sems, sem + 2, *beside))

    def start(self):
        for link in (*self.corner, *self.down):
            link.start()

    def blank(self):
        @pl.when(jnp.logical_not(self.has["up"]))
        def _():
            self.got[0:2] = jnp.zeros((2, *self.passing.shape), F32)

        @pl.when(jnp.logical_not(self.has["left"]))
        def _():
            self.got[2] = jnp.zeros(self.passing.shape, F32)

    def turn(self, plane):
        self.corner[plane].arrived()
        self.passing[plane] = self.quarters[1][plane] + self.got[0, plane]
        self.across[plane].start()

    def finish(self):
        for link in (*self.down, *self.across):
            link.arrived()
        for link in (*self.corner, *self.down, *self.across):
            link.sent()

    def total(self, plane):
        return self.quarters[0][plane] + self.got[1, plane] + self.got[2, plane]


def halo_kernel(own, region, *sems):
    has, where = neighbours()
    greet(has, where)
    halo = Halo(own, region, sems, 0, has, where)
    halo.start()
    halo.blank()
    for plane in range(own.shape[0]):
        halo.turn(plane)
    halo.finish()


def first_kernel(coords, live, region, probe, wave, *refs):
    *quarters, totals = refs
    totals[...] = jnp.zeros_like(totals)

    @pl.loop(0, coords.shape[0])
    def _(slot):
        top, left = coords[slot, 0], coords[slot, 1]
        real, imag = window(region, 0, top, left), window(region, 1, top, left)
        wave[slot, 0] = probe[0] * real - probe[1] * imag
        wave[slot, 1] = probe[0] * imag + probe[1] * real

        @pl.when(slot < live[0])
        def _():
            deposit(totals, 0, probe[0] * probe[0] + probe[1] * probe[1], top, left)

    write_quarters(totals, *quarters)


def double_transform(group, source, target, tables, between, after, hooks):
    steps = source.shape[0] // group

    @pl.loop(0, steps)
    def _(step):
        slots = [step * group + at for at in range(group)]
        spec_r, spec_i = forward(
            [source[slot, 0] for slot in slots], [source[slot, 1] for slot in slots], *tables
        )
        for at, hook in enumerate(hooks):
            if at % 2 == 0 and at // 2 < steps:
                pl.when(step == at // 2)(hook)
        moved = [between(slot, a, b) for slot, a, b in zip(slots, spec_r, spec_i)]
        out_r, minus_i = forward([m[0] for m in moved], [-m[1] for m in moved], *tables)
        for slot, a, b in zip(slots, out_r, minus_i):
            target[slot, 0], target[slot, 1] = after(a, -b)
        for at, hook in enumerate(hooks):
            if at % 2 == 1 and at // 2 < steps:
                pl.when(step == at // 2)(hook)

    for hook in hooks[2 * steps :]:
        hook()


def wave_kernel(group, source, own, n_ul, n_ur, n_ll, n_lr, phase, left_t, right_t, *refs):
    wave, region, norm_sum, passing, got, *sems = refs
    has, where = neighbours()
    greet(has, where)
    halo = Halo(own, region, sems, 0, has, where)
    sums = Sums((n_ul, n_ur, n_ll, n_lr), passing, got, sems, 3 * own.shape[0], has, where)
    halo.start()
    sums.start()
    halo.blank()
    sums.blank()

    def between(slot, real, imag):
        return real * phase[0] - imag * phase[1], real * phase[1] + imag * phase[0]

    hooks = [
        lambda: sums.turn(0),
        lambda: halo.turn(0),
        lambda: halo.turn(1),
    ]
    double_transform(
        group, source, wave, (left_t, right_t), between, lambda a, b: (a, b), hooks
    )
    halo.finish()
    sums.finish()
    norm_sum[...] = sums.total(0)


def second_kernel(coords, live, wave, region, exit_wave, patch, *refs):
    *quarters, totals = refs
    totals[...] = jnp.zeros_like(totals)

    @pl.loop(0, coords.shape[0])
    def _(slot):
        top, left = coords[slot, 0], coords[slot, 1]
        second_r, second_i = window(region, 0, top, left), window(region, 1, top, left)
        wave_r, wave_i = wave[slot, 0], wave[slot, 1]
        patch[slot, 0], patch[slot, 1] = second_r, second_i
        exit_wave[slot, 0] = wave_r * second_r - wave_i * second_i
        exit_wave[slot, 1] = wave_r * second_i + wave_i * second_r

        @pl.when(slot < live[0])
        def _():
            deposit(totals, 0, wave_r * wave_r + wave_i * wave_i, top, left)

    write_quarters(totals, *quarters)


def back_kernel(group, source, n_ul, n_ur, n_ll, n_lr, amplitude, left_t, right_t, *refs):
    back, norm_sum, passing, got, *sems = refs
    has, where = neighbours()
    greet(has, where)
    sums = Sums((n_ul, n_ur, n_ll, n_lr), passing, got, sems, 0, has, where)
    sums.start()
    sums.blank()

    def between(slot, real, imag):
        ratio = amplitude[slot] * jnp.minimum(lax.rsqrt(real * real + imag * imag), 2.0) - 1.0
        return real * ratio, imag * ratio

    double_transform(
        group,
        source,
        back,
        (left_t, right_t),
        between,
        lambda a, b: (a, b),
        [lambda: sums.turn(0)],
    )
    sums.finish()
    norm_sum[...] = sums.total(0)


def third_kernel(coords, live, wave, patch, back, inner, *refs):
    *quarters, totals = refs
    totals[...] = jnp.zeros_like(totals)

    @pl.loop(0, coords.shape[0])
    def _(slot):
        top, left = coords[slot, 0], coords[slot, 1]
        real, imag = back[slot, 0], back[slot, 1]
        second_r, second_i = patch[slot, 0], patch[slot, 1]
        inner[slot, 0] = second_r * real + second_i * imag
        inner[slot, 1] = second_r * imag - second_i * real

        @pl.when(slot < live[0])
        def _():
            wave_r, wave_i = wave[slot, 0], wave[slot, 1]
            deposit(totals, 0, wave_r * real + wave_i * imag, top, left)
            deposit(totals, 1, wave_r * imag - wave_i * real, top, left)

    write_quarters(totals, *quarters)


def grad_kernel(group, source, g_ul, g_ur, g_ll, g_lr, probe, phase, left_t, right_t, *refs):
    grad, grad_sum, passing, got, *sems = refs
    has, where = neighbours()
    greet(has, where)
    sums = Sums((g_ul, g_ur, g_ll, g_lr), passing, got, sems, 0, has, where)
    sums.start()
    sums.blank()

    def between(slot, real, imag):
        return real * phase[0] + imag * phase[1], imag * phase[0] - real * phase[1]

    def after(real, imag):
        return probe[0] * real + probe[1] * imag, probe[0] * imag - probe[1] * real

    double_transform(
        group,
        source,
        grad,
        (left_t, right_t),
        between,
        after,
        [lambda: sums.turn(0), lambda: sums.turn(1)],
    )
    sums.finish()
    for plane in range(2):
        grad_sum[plane] = sums.total(plane)


def fourth_kernel(coords, live, grad, *refs):
    *quarters, totals = refs
    totals[...] = jnp.zeros_like(totals)

    @pl.loop(0, live[0])
    def _(slot):
        top, left = coords[slot, 0], coords[slot, 1]
        deposit(totals, 0, grad[slot, 0], top, left)
        deposit(totals, 1, grad[slot, 1], top, left)

    write_quarters(totals, *quarters)


def last_kernel(g_ul, g_ur, g_ll, g_lr, *refs):
    grad_sum, passing, got, *sems = refs
    has, where = neighbours()
    greet(has, where)
    sums = Sums((g_ul, g_ur, g_ll, g_lr), passing, got, sems, 0, has, where)
    sums.start()
    sums.blank()
    for plane in range(2):
        sums.turn(plane)
    sums.finish()
    for plane in range(2):
        grad_sum[plane] = sums.total(plane)


def on_device(object_planes, probe, phase, coords, live, amplitude):
    width = probe.shape[-1]
    slots = coords.shape[2]
    group = 2 if slots % 2 == 0 else 1
    left_t, right_t = split_tables(width)
    phase_ri = jnp.stack([jnp.cos(phase), jnp.sin(phase)])
    place = (coords[0, 0], live[0])
    smem = pl.BlockSpec(memory_space=pltpu.SMEM)
    vmem = pl.BlockSpec(memory_space=pltpu.VMEM)

    def plane(*lead):
        return jax.ShapeDtypeStruct((*lead, width, width), F32)

    def double(planes):
        return jax.ShapeDtypeStruct((planes, 2 * width, 2 * width), F32)

    def totals(planes):
        return [pltpu.VMEM((planes, 2 * width, 2 * width), F32)]

    def wires(planes, links):
        sums = [pltpu.VMEM((planes, width, width), F32), pltpu.VMEM((3, planes, width, width), F32)]
        return (sums if planes else []) + [pltpu.SemaphoreType.DMA((links,))] * 2

    dots = 2 * slots * 2 * 2 * width * 2 * width * 6 * width

    def call(body, outs, scratches, name, scalars=0, ident=None, flops=1 << 20):
        def run(*args):
            return pl.pallas_call(
                body,
                out_shape=outs,
                in_specs=[smem] * scalars + [vmem] * (len(args) - scalars),
                out_specs=jax.tree.map(lambda _: vmem, outs),
                scratch_shapes=scratches,
                compiler_params=pltpu.CompilerParams(
                    vmem_limit_bytes=32 << 20,
                    collective_id=ident,
                    has_side_effects=ident is not None,
                ),
                cost_estimate=pl.CostEstimate(
                    flops=flops, bytes_accessed=8 << 20, transcendentals=0
                ),
                name=name,
            )(*args)

        return run

    def bind(body):
        def bound(*refs):
            body(group, *refs)

        return bound

    tables = (left_t, right_t)
    first, second = object_planes[0:2], object_planes[2:4]
    waves = plane(slots, 2)
    quarters = [plane(1)] * 4
    pairs = [plane(2)] * 4
    region_one = call(halo_kernel, double(2), wires(0, 6), "halo", ident=0)(first)
    incident, *norm_one = call(first_kernel, [waves, *quarters], totals(1), "first", 2)(
        *place, region_one, probe
    )
    wave, region_two, norm_one = call(
        bind(wave_kernel), [waves, double(2), plane()], wires(1, 9), "wave", ident=1, flops=dots
    )(incident, second, *norm_one, phase_ri, *tables)
    exit_wave, patch, *norm_two = call(
        second_kernel, [waves, waves, *quarters], totals(1), "second", 2
    )(*place, wave, region_two)
    back, norm_two = call(
        bind(back_kernel), [waves, plane()], wires(1, 3), "back", ident=2, flops=dots
    )(exit_wave, *norm_two, amplitude[0, 0], *tables)
    inner, *grad_two = call(third_kernel, [waves, *pairs], totals(2), "third", 2)(
        *place, wave, patch, back
    )
    grad, grad_two = call(
        bind(grad_kernel), [waves, plane(2)], wires(2, 6), "grad", ident=3, flops=dots
    )(inner, *grad_two, probe, phase_ri, *tables)
    grad_one = call(fourth_kernel, pairs, totals(2), "fourth", 2)(*place, grad)
    grad_one = call(last_kernel, plane(2), wires(2, 6), "last", ident=4)(*grad_one)
    new_first = first + grad_one / (norm_one + 1.0)
    new_second = second + grad_two / (norm_two + 1.0)
    return jnp.concatenate([new_first, new_second])


def solution(mesh):
    return jax.shard_map(
        on_device,
        mesh=mesh,
        in_specs=(
            P(None, ("groups", "ty"), "tx"),
            P(),
            P(),
            P(("groups", "ty"), "tx", None, None),
            P(("groups", "ty"), "tx"),
            P(("groups", "ty"), "tx", None, None, None),
        ),
        out_specs=P(None, ("groups", "ty"), "tx"),
        check_vma=False,
    )
```

time: 122 us -> 99.3 us (0.81)
  the two profiles are of different devices: /device:TPU:0 before, /device:TPU:22 now
where the time goes in v2:
time: 99.3 us; the launch traced here: 98.2 us
  Pallas kernels  90.5 us (91%)
  local copies, waits for them, and re-layouts  3.38 us (3%)
  other arithmetic  3.28 us (3%)
    pallas_call x9, Pallas kernels, run(): pl.pallas_call(body, out_shape=outs, in_specs=[smem] * scalars + [vmem] *...  90.5 us
    slice x1, other arithmetic, on_device(): first, second = (object_planes[0:2], object_planes[2:4])  2.1 us

profile of v2, /device:TPU:22, one launch (start us, length us, event | category | flops | bytes accessed | tf_op | source)
XLA Modules:
  0.0 98.2 jit_solution(17767267007807704752)
XLA Ops:
  0.0 1.9 %cosine_bitcast_fusion = (f32[1,256,256]{2,1,0:T(8,128)S(1)}, f32[1,256,256]{2,1,0:T(8,128)S(1)}) fusion(f32[256,256]{1,0:T(8,128)} %param.10), kind=kLoop, calls=%fused_computation.5 | loop fusion | bytes 786432 | tf_op jit(solution)/shard_map/stack | solution.py:451
  1.9 2.1 %fusion = (f32[2,256,256]{2,1,0:T(8,128)}, f32[2,256,256]{2,1,0:T(8,128)S(1)}, f32[2,256,256]{2,1,0:T(8,128)S(1)}) fusion(f32[4,256,256]{2,1,0:T(8,128)} %param.8, f32[1,256,256]{2,1,0:T(8,128)S(1)} %get-tuple-element.64, f32[1,256,256]{2,1,0:T(8,128)S(1)} %get-tuple-element.63), kind=kLoop, calls=%fused_computation.8 | loop fusion | flops 131072 | bytes 3145728 | tf_op jit(solution)/shard_map/slice | solution.py:499
  4.0 0.0 copy-start.7
  4.0 0.0 copy-start
  4.0 18.2 %halo.1.region = f32[2,512,512]{2,1,0:T(8,128)S(1)} custom-call(f32[2,256,256]{2,1,0:T(8,128)S(1)} %get-tuple-element.62.own), custom_call_target="tpu_custom_call" | custom-call | flops 1048576 | bytes 8388608 | tf_op jit(solution)/shard_map/halo/pallas_call | solution.py:473
  22.1 0.0 copy-done.7
  22.1 0.1 copy.12.coords
  22.2 0.0 copy-start.1
  22.2 0.0 copy-start.3
  23.0 0.0 copy-done
  23.1 3.5 %first.1 = (f32[4,2,256,256]{3,2,1,0:T(8,128)S(1)}, f32[1,256,256]{2,1,0:T(8,128)S(1)}, f32[1,256,256]{2,1,0:T(8,128)S(1)}, f32[1,256,256]{2,1,0:T(8,128)S(1)}, f32[1,256,256]{2,1,0:T(8,128)S(1)}) custom-call(s32[4,2]{1,0:T(4,128)S(1)} %copy.12.coords, s32[1]{0:T(128)} %bitcast.7.live, f32[2,512,512]{2,1,0:T(8,128)S(1)} %halo.1.region, ...), custom_call_target="tpu_custom_call" | custom-call | flops 1048576 | bytes 8388608 | tf_op jit(solution)/shard_map/first/pallas_call | solution.py:473
  26.5 0.0 copy-done.1
  26.5 0.0 copy-done.3
  26.5 0.0 copy-start.4
  26.6 1.4 %copy-done.4 = bf16[1536,512]{1,0:T(8,128)(2,1)S(1)} copy-done((bf16[1536,512]{1,0:T(8,128)(2,1)S(1)}, bf16[1536,512]{1,0:T(8,128)(2,1)}, u32[]{:S(2)}) %copy-start.4) | copy-done | bytes 1572888
  28.0 15.9 %wave.1 = (f32[4,2,256,256]{3,2,1,0:T(8,128)S(1)}, f32[2,512,512]{2,1,0:T(8,128)S(1)}, f32[256,256]{1,0:T(8,128)S(1)}) custom-call(f32[4,2,256,256]{3,2,1,0:T(8,128)S(1)} %get-tuple-element.32.refs_0_, f32[2,256,256]{2,1,0:T(8,128)S(1)} %copy-done.1, f32[1,256,256]{2,1,0:T(8,128)S(1)} %get-tuple-element.33.refs_2_, ...), custom_call_target="tpu_custom_call" | custom-call | flops 6442450944 | bytes 8388608 | tf_op jit(solution)/shard_map/wave/pallas_call | solution.py:473
  43.8 0.0 copy-start.2
  43.8 0.0 copy-start.5
  43.8 3.6 %second.1 = (f32[4,2,256,256]{3,2,1,0:T(8,128)S(1)}, f32[4,2,256,256]{3,2,1,0:T(8,128)S(1)}, f32[1,256,256]{2,1,0:T(8,128)S(1)}, f32[1,256,256]{2,1,0:T(8,128)S(...) custom-call(s32[4,2]{1,0:T(4,128)S(1)} %copy.12.coords, s32[1]{0:T(128)} %bitcast.8.live, ...), custom_call_target="tpu_custom_call" | custom-call | flops 1048576 | bytes 8388608 | tf_op jit(solution)/shard_map/second/pallas_call | solution.py:473
  47.4 0.0 copy-done.2
  47.4 0.0 copy-done.5
  47.5 14.7 %back.1 = (f32[4,2,256,256]{3,2,1,0:T(8,128)S(1)}, f32[256,256]{1,0:T(8,128)S(1)}) custom-call(f32[4,2,256,256]{3,2,1,0:T(8,128)S(1)} %get-tuple-element.40.refs_0_, f32[1,256,256]{2,1,0:T(8,128)S(1)} %get-tuple-element.41.refs_1_, f32[1,256,256]{2,1,0:T(8,128)S(1)} %get-tuple-element.42.refs_2_, f32[1,256,256]{2,1,0:T(8,128)S(1)} %get-tuple-element.43.refs_3_, ...), custom_call_target="tpu_custom_call" | custom-call | flops 6442450944 | bytes 8388608 | tf_op jit(solution)/shard_map/back/pallas_call | solution.py:473
  62.2 1.6 %third.1 = (f32[4,2,256,256]{3,2,1,0:T(8,128)S(1)}, f32[2,256,256]{2,1,0:T(8,128)S(1)}, f32[2,256,256]{2,1,0:T(8,128)S(1)}, f32[2,256,256]{2,1,0:T(8,128)S(1)}, f32[2,256,256]{2,1,0:T(8,128)S(1)}) custom-call(s32[4,2]{1,0:T(4,128)S(1)} %copy.12.coords, s32[1]{0:T(128)} %bitcast.9.live, f32[4,2,256,256]{3,2,1,0:T(8,128)S(1)} %get-tuple-element.37.wave, ...), custom_call_target="tpu_custom_call" | custom-call | flops 1048576 | bytes 8388608 | tf_op jit(solution)/shard_map/third/pallas_call | solution.py:473
  63.8 15.9 %grad.1 = (f32[4,2,256,256]{3,2,1,0:T(8,128)S(1)}, f32[2,256,256]{2,1,0:T(8,128)S(1)}) custom-call(f32[4,2,256,256]{3,2,1,0:T(8,128)S(1)} %get-tuple-element.46.refs_0_, f32[2,256,256]{2,1,0:T(8,128)S(1)} %get-tuple-element.47.refs_1_, f32[2,256,256]{2,1,0:T(8,128)S(1)} %get-tuple-element.48.refs_2_, f32[2,256,256]{2,1,0:T(8,128)S(1)} %get-tuple-element.49.refs_3_, ...), custom_call_target="tpu_custom_call" | custom-call | flops 6442450944 | bytes 8388608 | tf_op jit(solution)/shard_map/grad/pallas_call | solution.py:473
  79.8 1.2 %fourth.1 = (f32[2,256,256]{2,1,0:T(8,128)S(1)}, f32[2,256,256]{2,1,0:T(8,128)S(1)}, f32[2,256,256]{2,1,0:T(8,128)S(1)}, f32[2,256,256]{2,1,0:T(8,128)S(1)}) custom-call(s32[4,2]{1,0:T(4,128)S(1)} %copy.12.coords, s32[1]{0:T(128)} %bitcast.10.live, f32[4,2,256,256]{3,2,1,0:T(8,128)S(1)} %get-tuple-element.51.grad), custom_call_target="tpu_custom_call" | custom-call | flops 1048576 | bytes 8388608 | tf_op jit(solution)/shard_map/fourth/pallas_call | solution.py:473
  81.0 0.0 copy-start.6
  81.0 15.9 %last.1 = f32[2,256,256]{2,1,0:T(8,128)S(1)} custom-call(f32[2,256,256]{2,1,0:T(8,128)S(1)} %get-tuple-element.52.g_ul, f32[2,256,256]{2,1,0:T(8,128)S(1)} %get-tuple-element.53.g_ur, f32[2,256,256]{2,1,0:T(8,128)S(1)} %get-tuple-element.54.g_ll, f32[2,256,256]{2,1,0:T(8,128)S(1)} %get-tuple-element.55.g_lr), custom_call_target="tpu_custom_call" | custom-call | flops 1048576 | bytes 8388608 | tf_op jit(solution)/shard_map/last/pallas_call | solution.py:473
  97.0 0.0 copy-done.6
  97.0 1.1 %divide_add_fusion.1 = (f32[4,256,256]{2,1,0:T(8,128)}, f32[4,256,256]{2,1,0:T(8,128)}) fusion(f32[2,256,256]{2,1,0:T(8,128)S(1)} %last.1, f32[256,256]{1,0:T(8,128)S(1)} %broadcast_add_fusion.1, f32[4,256,256]{2,1,0:T(8,128)S(1)} %copy-done.6, f32[2,256,256]{2,1,0:T(8,128)S(1)} %get-tuple-element.57, ...), kind=kLoop, output_to_operand_aliasing={{0}: (5, {}), {1}: (5, {})}, calls=%fused_computation.3 | loop fusion | flops 524288 | bytes 3670016 | tf_op jit(solution)/shard_map/add | solution.py:524
  (3 shorter events, 0.0 us)
Async XLA Ops:
  4.0 18.2 %copy-start.7 = (s32[1,1,4,2]{2,3,1,0:T(2,128)S(1)}, s32[1,1,4,2]{2,3,1,0:T(2,128)}, u32[]{:S(2)}) copy-start(s32[1,1,4,2]{2,3,1,0:T(2,128)} %param.11) | copy-start | bytes 100
  4.0 19.1 %copy-start = (f32[2,256,256]{2,1,0:T(8,128)S(1)}, f32[2,256,256]{2,1,0:T(8,128)}, u32[]{:S(2)}) copy-start(f32[2,256,256]{2,1,0:T(8,128)} %refs_5_.1) | copy-start | bytes 1572868
  22.2 4.3 %copy-start.1 = (f32[2,256,256]{2,1,0:T(8,128)S(1)}, f32[2,256,256]{2,1,0:T(8,128)}, u32[]{:S(2)}) copy-start(f32[2,256,256]{2,1,0:T(8,128)} %get-tuple-element.61.refs_1_) | copy-start | bytes 1572868
  22.2 4.3 %copy-start.3 = (bf16[512,1536]{1,0:T(8,128)(2,1)S(1)}, bf16[512,1536]{1,0:T(8,128)(2,1)}, u32[]{:S(2)}) copy-start(bf16[512,1536]{1,0:T(8,128)(2,1)} %constant.6.clone.refs_7_.refs_6_) | copy-start | bytes 4718596
  26.5 1.4 %copy-start.4 = (bf16[1536,512]{1,0:T(8,128)(2,1)S(1)}, bf16[1536,512]{1,0:T(8,128)(2,1)}, u32[]{:S(2)}) copy-start(bf16[1536,512]{1,0:T(8,128)(2,1)} %constant.7.clone.refs_8_.refs_7_) | copy-start | bytes 4718596
  43.8 3.6 %copy-start.2 = (f32[1,1,4,256,256]{4,3,2,1,0:T(8,128)S(1)}, f32[1,1,4,256,256]{4,3,2,1,0:T(8,128)}, u32[]{:S(2)}) copy-start(f32[1,1,4,256,256]{4,3,2,1,0:T(8,128)} %param.13) | copy-start | bytes 3145732
  43.8 3.6 %copy-start.5 = (bf16[1536,512]{1,0:T(8,128)(2,1)S(1)}, bf16[1536,512]{1,0:T(8,128)(2,1)}, u32[]{:S(2)}) copy-start(bf16[1536,512]{1,0:T(8,128)(2,1)} %constant.7.clone.refs_8_.refs_7_) | copy-start | bytes 4718596
  81.0 16.0 %copy-start.6 = (f32[4,256,256]{2,1,0:T(8,128)S(1)}, f32[4,256,256]{2,1,0:T(8,128)}, u32[]{:S(2)}) copy-start(f32[4,256,256]{2,1,0:T(8,128)} %param.8) | copy-start | bytes 3145732

commit v3 on v2

--- a/solution.py
+++ b/solution.py
@@ -31,7 +31,7 @@
         ],
         axis=0,
     )
-    return jnp.asarray(left), jnp.asarray(np.ascontiguousarray(left.T))
+    return jnp.asarray(left)
 
 
 def split(value):
@@ -164,10 +164,6 @@
             )
             self.corner.append(Link(right, beyond, sems, sem + 2, where["up"], *both))
 
-    def start(self):
-        for link in (*self.across, *self.down):
-            link.start()
-
     def blank(self):
         has, region, width = self.has, self.region, self.own.shape[-1]
         upper, lower = slice(0, width), slice(width, 2 * width)
@@ -190,10 +186,10 @@
         self.across[plane].arrived()
         self.corner[plane].start()
 
-    def finish(self):
+    def finish(self, start):
         for link in (*self.down, *self.corner):
             link.arrived()
-        for link in (*self.across, *self.down, *self.corner):
+        for link in (*self.across[start:], *self.down, *self.corner):
             link.sent()
 
 
@@ -215,8 +211,7 @@
             self.across.append(Link(passing.at[plane], got.at[2, plane], sems, sem + 2, *beside))
 
     def start(self):
-        for link in (*self.corner, *self.down):
-            link.start()
+        self.corner[0].start()
 
     def blank(self):
         @pl.when(jnp.logical_not(self.has["up"]))
@@ -229,6 +224,8 @@
 
     def turn(self, plane):
         self.corner[plane].arrived()
+        for link in self.corner[plane + 1 : plane + 2] or self.down:
+            link.start()
         self.passing[plane] = self.quarters[1][plane] + self.got[0, plane]
         self.across[plane].start()
 
@@ -242,44 +239,43 @@
         return self.quarters[0][plane] + self.got[1, plane] + self.got[2, plane]
 
 
-def halo_kernel(own, region, *sems):
-    has, where = neighbours()
-    greet(has, where)
-    halo = Halo(own, region, sems, 0, has, where)
-    halo.start()
-    halo.blank()
-    for plane in range(own.shape[0]):
-        halo.turn(plane)
-    halo.finish()
-
-
-def first_kernel(coords, live, region, probe, wave, *refs):
-    *quarters, totals = refs
-    totals[...] = jnp.zeros_like(totals)
-
-    @pl.loop(0, coords.shape[0])
-    def _(slot):
-        top, left = coords[slot, 0], coords[slot, 1]
-        real, imag = window(region, 0, top, left), window(region, 1, top, left)
-        wave[slot, 0] = probe[0] * real - probe[1] * imag
-        wave[slot, 1] = probe[0] * imag + probe[1] * real
-
-        @pl.when(slot < live[0])
-        def _():
-            deposit(totals, 0, probe[0] * probe[0] + probe[1] * probe[1], top, left)
-
-    write_quarters(totals, *quarters)
-
-
-def double_transform(group, source, target, tables, between, after, hooks):
-    steps = source.shape[0] // group
+def turn_of(phase):
+    half = phase * 0.5
+    square = half * half
+    for at in range(7, -1, -1):
+        sign = -1.0 if at % 2 else 1.0
+        if at == 7:
+            cosine, sine = sign * (1.0 / math.factorial(14)), sign * (1.0 / math.factorial(15))
+        else:
+            cosine = cosine * square + sign / math.factorial(2 * at)
+            sine = sine * square + sign / math.factorial(2 * at + 1)
+    sine = sine * half
+    return 1.0 - 2.0 * sine * sine, 2.0 * sine * cosine
+
+
+def cut(parts, top, left):
+    tall, wide = parts.shape[0], parts.shape[0]
+    width = tall // 2
+    row = lax.broadcasted_iota(jnp.int32, (width, tall), 0)
+    column = lax.broadcasted_iota(jnp.int32, (width, tall), 1)
+    pick = jnp.where(column - row == top, 1.0, 0.0).astype(BF16)
+    rows = jnp.dot(pick, parts[...], preferred_element_type=F32).astype(BF16)
+    rows = jnp.concatenate([rows[:, : 2 * wide], rows[:, 2 * wide :]], axis=0)
+    row = lax.broadcasted_iota(jnp.int32, (wide, width), 0)
+    column = lax.broadcasted_iota(jnp.int32, (wide, width), 1)
+    pick = jnp.where(row - column == left, 1.0, 0.0).astype(BF16)
+    both = jnp.dot(rows, jnp.concatenate([pick, pick], axis=0), preferred_element_type=F32)
+    return both[:width], both[width:]
+
+
+def double_transform(group, count, source, target, tables, between, after, hooks):
+    steps = count // group
 
     @pl.loop(0, steps)
     def _(step):
         slots = [step * group + at for at in range(group)]
-        spec_r, spec_i = forward(
-            [source[slot, 0] for slot in slots], [source[slot, 1] for slot in slots], *tables
-        )
+        inputs = [source(slot) for slot in slots]
+        spec_r, spec_i = forward([a for a, _ in inputs], [b for _, b in inputs], *tables)
         for at, hook in enumerate(hooks):
             if at % 2 == 0 and at // 2 < steps:
                 pl.when(step == at // 2)(hook)
@@ -295,34 +291,61 @@
         hook()
 
 
-def wave_kernel(group, source, own, n_ul, n_ur, n_ll, n_lr, phase, left_t, right_t, *refs):
-    wave, region, norm_sum, passing, got, *sems = refs
+def wave_kernel(group, coords, own, probe, phase, left_t, *refs):
+    wave, region_two, right_t, phase_ri, region_one, parts, *sems = refs
+    width = own.shape[-1]
     has, where = neighbours()
     greet(has, where)
-    halo = Halo(own, region, sems, 0, has, where)
-    sums = Sums((n_ul, n_ur, n_ll, n_lr), passing, got, sems, 3 * own.shape[0], has, where)
-    halo.start()
-    sums.start()
-    halo.blank()
-    sums.blank()
+    one = Halo(own.at[0:2], region_one, sems, 0, has, where)
+    two = Halo(own.at[2:4], region_two, sems, 6, has, where)
+    one.across[0].start()
+    one.down[0].start()
+    one.down[1].start()
+    one.blank()
+    two.blank()
+    for at in range(6):
+        rows = slice(at * width, (at + 1) * width)
+        right_t[rows, :width] = left_t[:width, rows]
+        right_t[rows, width:] = left_t[width:, rows]
+    phase_ri[0], phase_ri[1] = turn_of(phase[...])
+    one.across[0].sent()
+    one.across[1].start()
+    one.turn(0)
+    one.across[1].sent()
+    two.across[0].start()
+    one.turn(1)
+    one.finish(start=2)
+    tall = 2 * width
+    for plane in range(2):
+        high, low = split(region_one[plane])
+        parts[:, 2 * plane * tall : (2 * plane + 1) * tall] = high
+        parts[:, (2 * plane + 1) * tall : (2 * plane + 2) * tall] = low
+
+    def source(slot):
+        real, imag = cut(parts, coords[slot, 0], coords[slot, 1])
+        return probe[0] * real - probe[1] * imag, probe[0] * imag + probe[1] * real
 
     def between(slot, real, imag):
-        return real * phase[0] - imag * phase[1], real * phase[1] + imag * phase[0]
-
-    hooks = [
-        lambda: sums.turn(0),
-        lambda: halo.turn(0),
-        lambda: halo.turn(1),
-    ]
+        return (
+            real * phase_ri[0] - imag * phase_ri[1],
+            real * phase_ri[1] + imag * phase_ri[0],
+        )
+
+    def second_part():
+        two.across[0].sent()
+        two.across[1].start()
+        two.down[0].start()
+        two.down[1].start()
+
+    hooks = [second_part, lambda: two.turn(0), lambda: two.turn(1)]
+    count = coords.shape[0]
     double_transform(
-        group, source, wave, (left_t, right_t), between, lambda a, b: (a, b), hooks
+        group, count, source, wave, (left_t, right_t), between, lambda a, b: (a, b), hooks
     )
-    halo.finish()
-    sums.finish()
-    norm_sum[...] = sums.total(0)
-
-
-def second_kernel(coords, live, wave, region, exit_wave, patch, *refs):
+    two.finish(start=1)
+
+
+def second_kernel(coords, live, probe, wave, region, exit_wave, patch, *refs):
     *quarters, totals = refs
     totals[...] = jnp.zeros_like(totals)
 
@@ -337,7 +360,8 @@
 
         @pl.when(slot < live[0])
         def _():
-            deposit(totals, 0, wave_r * wave_r + wave_i * wave_i, top, left)
+            deposit(totals, 0, probe[0] * probe[0] + probe[1] * probe[1], top, left)
+            deposit(totals, 1, wave_r * wave_r + wave_i * wave_i, top, left)
 
     write_quarters(totals, *quarters)
 
@@ -356,15 +380,17 @@
 
     double_transform(
         group,
-        source,
+        source.shape[0],
+        lambda slot: (source[slot, 0], source[slot, 1]),
         back,
         (left_t, right_t),
         between,
         lambda a, b: (a, b),
-        [lambda: sums.turn(0)],
+        [lambda: sums.turn(0), lambda: sums.turn(1)],
     )
     sums.finish()
-    norm_sum[...] = sums.total(0)
+    for plane in range(2):
+        norm_sum[plane] = sums.total(plane)
 
 
 def third_kernel(coords, live, wave, patch, back, inner, *refs):
@@ -404,7 +430,8 @@
 
     double_transform(
         group,
-        source,
+        source.shape[0],
+        lambda slot: (source[slot, 0], source[slot, 1]),
         grad,
         (left_t, right_t),
         between,
@@ -436,10 +463,10 @@
     sums = Sums((g_ul, g_ur, g_ll, g_lr), passing, got, sems, 0, has, where)
     sums.start()
     sums.blank()
-    for plane in range(2):
+    for plane in range(g_ul.shape[0]):
         sums.turn(plane)
     sums.finish()
-    for plane in range(2):
+    for plane in range(g_ul.shape[0]):
         grad_sum[plane] = sums.total(plane)
 
 
@@ -447,8 +474,7 @@
     width = probe.shape[-1]
     slots = coords.shape[2]
     group = 2 if slots % 2 == 0 else 1
-    left_t, right_t = split_tables(width)
-    phase_ri = jnp.stack([jnp.cos(phase), jnp.sin(phase)])
+    left_t = split_tables(width)
     place = (coords[0, 0], live[0])
     smem = pl.BlockSpec(memory_space=pltpu.SMEM)
     vmem = pl.BlockSpec(memory_space=pltpu.VMEM)
@@ -462,9 +488,13 @@
     def totals(planes):
         return [pltpu.VMEM((planes, 2 * width, 2 * width), F32)]
 
-    def wires(planes, links):
-        sums = [pltpu.VMEM((planes, width, width), F32), pltpu.VMEM((3, planes, width, width), F32)]
-        return (sums if planes else []) + [pltpu.SemaphoreType.DMA((links,))] * 2
+    def wires(lead, rows, links):
+        return [
+            pltpu.VMEM((lead, rows, width), F32),
+            pltpu.VMEM((3, lead, rows, width), F32),
+            pltpu.SemaphoreType.DMA((links,)),
+            pltpu.SemaphoreType.DMA((links,)),
+        ]
 
     dots = 2 * slots * 2 * 2 * width * 2 * width * 6 * width
 
@@ -495,34 +525,48 @@
 
         return bound
 
-    tables = (left_t, right_t)
     first, second = object_planes[0:2], object_planes[2:4]
     waves = plane(slots, 2)
-    quarters = [plane(1)] * 4
     pairs = [plane(2)] * 4
-    region_one = call(halo_kernel, double(2), wires(0, 6), "halo", ident=0)(first)
-    incident, *norm_one = call(first_kernel, [waves, *quarters], totals(1), "first", 2)(
-        *place, region_one, probe
-    )
-    wave, region_two, norm_one = call(
-        bind(wave_kernel), [waves, double(2), plane()], wires(1, 9), "wave", ident=1, flops=dots
-    )(incident, second, *norm_one, phase_ri, *tables)
-    exit_wave, patch, *norm_two = call(
-        second_kernel, [waves, waves, *quarters], totals(1), "second", 2
-    )(*place, wave, region_two)
-    back, norm_two = call(
-        bind(back_kernel), [waves, plane()], wires(1, 3), "back", ident=2, flops=dots
-    )(exit_wave, *norm_two, amplitude[0, 0], *tables)
+    turned = jax.ShapeDtypeStruct((6 * width, 2 * width), BF16)
+    wave, region_two, right_t, phase_ri = call(
+        bind(wave_kernel),
+        [waves, double(2), turned, plane(2)],
+        [
+            *totals(2),
+            pltpu.VMEM((2 * width, 8 * width), BF16),
+            pltpu.SemaphoreType.DMA((12,)),
+            pltpu.SemaphoreType.DMA((12,)),
+        ],
+        "wave",
+        1,
+        ident=0,
+        flops=dots,
+    )(place[0], object_planes, probe, phase, left_t)
+    tables = (left_t, right_t)
+    exit_wave, patch, *norms = call(
+        second_kernel, [waves, waves, *pairs], totals(2), "second", 2
+    )(*place, probe, wave, region_two)
+    back, norms = call(
+        bind(back_kernel), [waves, plane(2)], wires(2, width, 6), "back", ident=1, flops=dots
+    )(exit_wave, *norms, amplitude[0, 0], *tables)
     inner, *grad_two = call(third_kernel, [waves, *pairs], totals(2), "third", 2)(
         *place, wave, patch, back
     )
     grad, grad_two = call(
-        bind(grad_kernel), [waves, plane(2)], wires(2, 6), "grad", ident=3, flops=dots
+        bind(grad_kernel), [waves, plane(2)], wires(2, width, 6), "grad", ident=2, flops=dots
     )(inner, *grad_two, probe, phase_ri, *tables)
     grad_one = call(fourth_kernel, pairs, totals(2), "fourth", 2)(*place, grad)
-    grad_one = call(last_kernel, plane(2), wires(2, 6), "last", ident=4)(*grad_one)
-    new_first = first + grad_one / (norm_one + 1.0)
-    new_second = second + grad_two / (norm_two + 1.0)
+    halves = (4, width // 2, width)
+    grad_one = call(
+        last_kernel,
+        jax.ShapeDtypeStruct(halves, F32),
+        wires(4, width // 2, 12),
+        "last",
+        ident=3,
+    )(*[quarter.reshape(halves) for quarter in grad_one]).reshape(2, width, width)
+    new_first = first + grad_one / (norms[0:1] + 1.0)
+    new_second = second + grad_two / (norms[1:2] + 1.0)
     return jnp.concatenate([new_first, new_second])
 
 

time: 99.3 us -> 104 us (1.047)
  Pallas kernels: 90.5 us -> 94.7 us
  other arithmetic: 3.28 us -> 1.18 us
  local copies, waits for them, and re-layouts: 3.38 us -> 5.41 us
    pallas_call x9 -> x7, Pallas kernels: 90.5 us -> 94.7 us  [run(): pl.pallas_call(body, out_shape=outs, in_specs=[smem] * scalars + [vmem] *...]
    unnamed x16, local copies, waits for them, and re-layouts: 1.44 us -> 4.65 us
    slice x1 -> x0, other arithmetic: 2.1 us -> none  [on_device(): first, second = (object_planes[0:2], object_planes[2:4])]
    another operation x1 -> x0, local copies, waits for them, and re-layouts: 1.85 us -> none  [on_device(): phase_ri = jnp.stack([jnp.cos(phase), jnp.sin(phase)])]
where the time goes in v3:
time: 104 us; the launch traced here: 102 us
  Pallas kernels  94.7 us (91%)
  local copies, waits for them, and re-layouts  5.41 us (5%)
  other arithmetic  1.18 us (1%)
    pallas_call x7, Pallas kernels, run(): pl.pallas_call(body, out_shape=outs, in_specs=[smem] * scalars + [vmem] *...  94.7 us
    unnamed x16, local copies, waits for them, and re-layouts  4.65 us

profile of v3, /device:TPU:22, one launch (start us, length us, event | category | flops | bytes accessed | tf_op | source)
XLA Modules:
  0.0 102.1 jit_solution(16323540328713749570)
XLA Ops:
  0.0 0.8 copy.11.refs_0_.coords
  0.8 0.0 copy-start
  0.8 1.2 %copy-done = f32[4,256,256]{2,1,0:T(8,128)S(1)} copy-done((f32[4,256,256]{2,1,0:T(8,128)S(1)}, f32[4,256,256]{2,1,0:T(8,128)}, u32[]{:S(2)}) %copy-start) | copy-done | bytes 1048600
  2.0 0.0 copy-start.2
  2.0 1.0 %copy-done.2 = f32[2,256,256]{2,1,0:T(8,128)S(1)} copy-done((f32[2,256,256]{2,1,0:T(8,128)S(1)}, f32[2,256,256]{2,1,0:T(8,128)}, u32[]{:S(2)}) %copy-start.2) | copy-done | bytes 524312
  3.0 0.0 copy-start.5
  3.0 0.9 copy-done.5
  4.0 0.0 copy-start.6
  4.0 1.4 %copy-done.6 = bf16[512,1536]{1,0:T(8,128)(2,1)S(1)} copy-done((bf16[512,1536]{1,0:T(8,128)(2,1)S(1)}, bf16[512,1536]{1,0:T(8,128)(2,1)}, u32[]{:S(2)}) %copy-start.6) | copy-done | bytes 1572888
  5.4 36.0 %wave.1 = (f32[4,2,256,256]{3,2,1,0:T(8,128)S(1)}, f32[2,512,512]{2,1,0:T(8,128)S(1)}, bf16[1536,512]{1,0:T(8,128)(2,1)S(1)}, f32[2,256,256]{2,1,0:T(8,128)S(1)}) custom-call(s32[4,2]{1,0:T(4,128)S(1)} %copy.11.refs_0_.coords, f32[4,256,256]{2,1,0:T(8,128)S(1)} %copy-done, f32[2,256,256]{2,1,0:T(8,128)S(1)} %copy-done.2, f32[256,256]{1,0:T(8,128)S(1)} %copy-done.5, ...), custom_call_target="tpu_custom_call" | custom-call | flops 6442450944 | bytes 8388608 | tf_op jit(solution)/shard_map/wave/pallas_call | solution.py:503
  42.0 0.0 copy-start.4
  42.1 0.0 copy-start.7
  42.1 4.4 %second.1 = (f32[4,2,256,256]{3,2,1,0:T(8,128)S(1)}, f32[4,2,256,256]{3,2,1,0:T(8,128)S(1)}, f32[2,256,256]{2,1,0:T(8,128)S(1)}, f32[2,256,256]{2,1,0:T(8,128)S(...) custom-call(s32[4,2]{1,0:T(4,128)S(1)} %copy.11.refs_0_.coords, s32[1]{0:T(128)} %bitcast.16.live, ...), custom_call_target="tpu_custom_call" | custom-call | flops 1048576 | bytes 8388608 | tf_op jit(solution)/shard_map/second/pallas_call | solution.py:503
  46.4 0.0 copy-done.4
  46.5 0.0 copy-done.7
  46.5 18.0 %back.1 = (f32[4,2,256,256]{3,2,1,0:T(8,128)S(1)}, f32[2,256,256]{2,1,0:T(8,128)S(1)}) custom-call(f32[4,2,256,256]{3,2,1,0:T(8,128)S(1)} %get-tuple-element.31.refs_0_, f32[2,256,256]{2,1,0:T(8,128)S(1)} %get-tuple-element.32.refs_1_, f32[2,256,256]{2,1,0:T(8,128)S(1)} %get-tuple-element.33.refs_2_, f32[2,256,256]{2,1,0:T(8,128)S(1)} %get-tuple-element.34.refs_3_, ...), custom_call_target="tpu_custom_call" | custom-call | flops 6442450944 | bytes 8388608 | tf_op jit(solution)/shard_map/back/pallas_call | solution.py:503
  64.4 0.0 copy-start.3
  64.4 2.2 %third.1 = (f32[4,2,256,256]{3,2,1,0:T(8,128)S(1)}, f32[2,256,256]{2,1,0:T(8,128)S(1)}, f32[2,256,256]{2,1,0:T(8,128)S(1)}, f32[2,256,256]{2,1,0:T(8,128)S(1)}, f32[2,256,256]{2,1,0:T(8,128)S(1)}) custom-call(s32[4,2]{1,0:T(4,128)S(1)} %copy.11.refs_0_.coords, s32[1]{0:T(128)} %bitcast.17.live, f32[4,2,256,256]{3,2,1,0:T(8,128)S(1)} %get-tuple-element.28.wave, ...), custom_call_target="tpu_custom_call" | custom-call | flops 1048576 | bytes 8388608 | tf_op jit(solution)/shard_map/third/pallas_call | solution.py:503
  66.6 0.0 copy-done.3
  66.6 16.7 %grad.1 = (f32[4,2,256,256]{3,2,1,0:T(8,128)S(1)}, f32[2,256,256]{2,1,0:T(8,128)S(1)}) custom-call(f32[4,2,256,256]{3,2,1,0:T(8,128)S(1)} %get-tuple-element.38.refs_0_, f32[2,256,256]{2,1,0:T(8,128)S(1)} %get-tuple-element.39.refs_1_, f32[2,256,256]{2,1,0:T(8,128)S(1)} %get-tuple-element.40.refs_2_, f32[2,256,256]{2,1,0:T(8,128)S(1)} %get-tuple-element.41.refs_3_, ...), custom_call_target="tpu_custom_call" | custom-call | flops 6442450944 | bytes 8388608 | tf_op jit(solution)/shard_map/grad/pallas_call | solution.py:503
  83.4 1.6 %fourth.1 = (f32[2,256,256]{2,1,0:T(8,128)S(1)}, f32[2,256,256]{2,1,0:T(8,128)S(1)}, f32[2,256,256]{2,1,0:T(8,128)S(1)}, f32[2,256,256]{2,1,0:T(8,128)S(1)}) custom-call(s32[4,2]{1,0:T(4,128)S(1)} %copy.11.refs_0_.coords, s32[1]{0:T(128)} %bitcast.18.live, f32[4,2,256,256]{3,2,1,0:T(8,128)S(1)} %get-tuple-element.44.grad), custom_call_target="tpu_custom_call" | custom-call | flops 1048576 | bytes 8388608 | tf_op jit(solution)/shard_map/fourth/pallas_call | solution.py:503
  85.0 0.0 copy-start.1
  85.0 15.9 %last.1 = f32[4,128,256]{2,1,0:T(8,128)S(1)} custom-call(f32[4,128,256]{2,1,0:T(8,128)S(1)} %bitcast.20, f32[4,128,256]{2,1,0:T(8,128)S(1)} %bitcast.21, f32[4,128,256]{2,1,0:T(8,128)S(1)} %bitcast.22, f32[4,128,256]{2,1,0:T(8,128)S(1)} %bitcast.23), custom_call_target="tpu_custom_call" | custom-call | flops 1048576 | bytes 8388608 | tf_op jit(solution)/shard_map/last/pallas_call | solution.py:503
  101.0 0.0 copy-done.1
  101.0 1.1 %fusion = (f32[4,256,256]{2,1,0:T(8,128)}, f32[4,256,256]{2,1,0:T(8,128)}) fusion(f32[4,256,256]{2,1,0:T(8,128)S(1)} %copy-done.1, f32[256,256]{1,0:T(8,128)S(1)} %get-tuple-element.53, f32[2,256,256]{2,1,0:T(8,128)S(1)} %get-tuple-element.50, f32[256,256]{1,0:T(8,128)S(1)} %get-tuple-element.54, ...), kind=kLoop, output_to_operand_aliasing={{0}: (5, {}), {1}: (5, {})}, calls=%fused_computation.2 | loop fusion | flops 524288 | bytes 3670016 | tf_op jit(solution)/shard_map/add | solution.py:568
  (2 shorter events, 0.0 us)
Async XLA Ops:
  0.8 1.2 %copy-start = (f32[4,256,256]{2,1,0:T(8,128)S(1)}, f32[4,256,256]{2,1,0:T(8,128)}, u32[]{:S(2)}) copy-start(f32[4,256,256]{2,1,0:T(8,128)} %refs_1_.1) | copy-start | bytes 3145732
  2.0 1.0 %copy-start.2 = (f32[2,256,256]{2,1,0:T(8,128)S(1)}, f32[2,256,256]{2,1,0:T(8,128)}, u32[]{:S(2)}) copy-start(f32[2,256,256]{2,1,0:T(8,128)} %refs_5_.1) | copy-start | bytes 1572868
  3.0 0.9 copy-start.5
  4.0 1.4 %copy-start.6 = (bf16[512,1536]{1,0:T(8,128)(2,1)S(1)}, bf16[512,1536]{1,0:T(8,128)(2,1)}, u32[]{:S(2)}) copy-start(bf16[512,1536]{1,0:T(8,128)(2,1)} %constant.4.clone.refs_4_.refs_6_.refs_7_) | copy-start | bytes 4718596
  42.0 4.4 %copy-start.4 = (f32[1,1,4,256,256]{4,3,2,1,0:T(8,128)S(1)}, f32[1,1,4,256,256]{4,3,2,1,0:T(8,128)}, u32[]{:S(2)}) copy-start(f32[1,1,4,256,256]{4,3,2,1,0:T(8,128)} %param.12) | copy-start | bytes 3145732
  42.1 4.4 %copy-start.7 = (bf16[512,1536]{1,0:T(8,128)(2,1)S(1)}, bf16[512,1536]{1,0:T(8,128)(2,1)}, u32[]{:S(2)}) copy-start(bf16[512,1536]{1,0:T(8,128)(2,1)} %constant.4.clone.refs_4_.refs_6_.refs_7_) | copy-start | bytes 4718596
  64.4 2.2 %copy-start.3 = (f32[2,256,256]{2,1,0:T(8,128)S(1)}, f32[2,256,256]{2,1,0:T(8,128)}, u32[]{:S(2)}) copy-start(f32[2,256,256]{2,1,0:T(8,128)} %refs_5_.1) | copy-start | bytes 1572868
  85.0 16.0 %copy-start.1 = (f32[4,256,256]{2,1,0:T(8,128)S(1)}, f32[4,256,256]{2,1,0:T(8,128)}, u32[]{:S(2)}) copy-start(f32[4,256,256]{2,1,0:T(8,128)} %refs_1_.1) | copy-start | bytes 3145732
